TPU v7x, 256 devices: a whole 4x4x8 slice. The times are simulated.
256 devices in a mesh: bx: 32 (over z, x), by: 8 (over y, core).
Axes of the slice: x: 4, y: 4, z: 8, core: 2. Of those that a mesh axis runs over, the one named last changes fastest.
Arguments:
- scalar_field: float32 [64, 1024, 1024], P(None, 'bx', 'by'), may hold values from -8 to 8
- transfer_in: bfloat16 [16, 8], replicated, may hold values from -2 to 2
- transfer_out: bfloat16 [16, 16], replicated, may hold values from -1.5 to 1.5
Outputs:
- view_x: float32 [2, 8, 64, 1024], P(None, None, 'bx', 'by')
- view_y: float32 [2, 8, 64, 1024], P(None, None, 'by', 'bx')
All inputs are finite; a program needn't handle non-finite values.
Results may differ from a plain program's by a relative error of at most 0.00035.
Values sent between devices are 32-bit elements; how exact they have to be, the bound alone decides.
A program may use at most 64 MiB of HBM per device.

v0:
```python
import jax
import jax.numpy as jnp
from jax import lax
from jax.sharding import PartitionSpec as P


def extended_2(shard, sides, width):
    for axis, dim in sides:
        peers, length = (lax.axis_size(axis), shard.shape[dim])
        up = [(i, (i + 1) % peers) for i in range(peers - 1)]
        down = [(j, i) for i, j in up]
        last = lax.slice_in_dim(shard, length - width, length, axis=dim)
        initial = lax.slice_in_dim(shard, 0, width, axis=dim)
        before = lax.ppermute(last, axis, up)
        after = lax.ppermute(initial, axis, down)
        shard = jnp.concatenate([before, shard, after], axis=dim)
    return shard


def entering(part, axis, combine, identity, reverse):
    count = lax.axis_size(axis)
    place = lax.axis_index(axis)
    ahead = count - 1 - place if reverse else place
    gathered = jax.tree.map(lambda a: lax.all_gather(a, axis), part)
    state = jax.tree.map(lambda a, e: jnp.zeros_like(a) + jnp.asarray(e, a.dtype), part, identity)

    def one(hop, state):
        source = count - 1 - hop if reverse else hop
        return combine(
            state, jax.tree.map(lambda a: lax.dynamic_index_in_dim(a, source, 0, False), gathered)
        )

    return lax.fori_loop(0, ahead, one, state)


def smooth_inner(extended):
    centre = extended[:, 1:-1, 1:-1]
    padded_z = jnp.pad(centre, ((1, 1), (0, 0), (0, 0)))
    nearby = (
        extended[:, 2:, 1:-1]
        + extended[:, :-2, 1:-1]
        + extended[:, 1:-1, 2:]
        + extended[:, 1:-1, :-2]
    )
    nearby = nearby + padded_z[2:] + padded_z[:-2]
    return 0.4 * centre + 0.1 * nearby


def plain_rim(values):
    return extended_2(values, (("bx", 1), ("by", 2)), 1)


def upper_ones(length):
    rows_at = lax.broadcasted_iota(jnp.int32, (length, length), 0)
    cols_at = lax.broadcasted_iota(jnp.int32, (length, length), 1)
    return (rows_at <= cols_at).astype(jnp.float32)


def gradients(padded):
    diff_x = padded[:, 2:, :] - padded[:, :-2, :]
    grad_x = (
        2.0 * diff_x[1:-1, :, 1:-1]
        + diff_x[:-2, :, 1:-1]
        + diff_x[2:, :, 1:-1]
        + diff_x[1:-1, :, :-2]
        + diff_x[1:-1, :, 2:]
    ) / 12.0
    diff_y = padded[:, :, 2:] - padded[:, :, :-2]
    grad_y = (
        2.0 * diff_y[1:-1, 1:-1]
        + diff_y[:-2, 1:-1]
        + diff_y[2:, 1:-1]
        + diff_y[1:-1, :-2]
        + diff_y[1:-1, 2:]
    ) / 12.0
    diff_z = padded[2:] - padded[:-2]
    grad_z = (
        2.0 * diff_z[:, 1:-1, 1:-1]
        + diff_z[:, :-2, 1:-1]
        + diff_z[:, 2:, 1:-1]
        + diff_z[:, 1:-1, :-2]
        + diff_z[:, 1:-1, 2:]
    ) / 12.0
    return (padded[1:-1, 1:-1, 1:-1], grad_x, grad_y, grad_z)


def transfer(padded, transfer_in, transfer_out, bands):
    centre, grad_x, grad_y, grad_z = gradients(padded)
    scaled_x = 4.0 * grad_x
    scaled_y = 4.0 * grad_y
    scaled_z = 4.0 * grad_z
    magnitude = jnp.sqrt(1.0 + scaled_x * scaled_x + scaled_y * scaled_y + scaled_z * scaled_z)
    features = jnp.stack(
        [
            centre,
            scaled_x,
            scaled_y,
            scaled_z,
            magnitude,
            centre * magnitude,
            centre * centre,
            jnp.ones_like(centre),
        ]
    ).astype(jnp.bfloat16)
    hidden = jax.nn.silu(
        jnp.einsum("hf,fzxy->hzxy", transfer_in, features, preferred_element_type=jnp.float32)
    ).astype(jnp.bfloat16)
    channels = jnp.einsum("ch,hzxy->czxy", transfer_out, hidden, preferred_element_type=jnp.float32)
    return (jax.nn.softplus(channels[:bands]), jax.nn.softplus(channels[bands:]))


def composite(ahead_pair, later_pair):
    return (ahead_pair[0] + ahead_pair[1] * later_pair[0], ahead_pair[1] * later_pair[1])


def composite_back(earlier, later):
    return composite(later, earlier)


def fold_bricks(pieces):
    clearance = pieces[:, 1]
    leading = jnp.ones_like(clearance[:1])
    shading = jnp.cumprod(jnp.concatenate([leading, clearance[:-1]], axis=0), axis=0)
    colour = jnp.sum(shading * pieces[:, 0], axis=0)
    return jnp.stack([colour, shading[-1] * clearance[-1]])


def body(scalar_field, transfer_in, transfer_out):
    layers, local_x, local_y = scalar_field.shape
    bands = transfer_out.shape[0] // 2
    count_x = lax.axis_size("bx")
    count_y = lax.axis_size("by")
    full_x = local_x * count_x
    full_y = local_y * count_y
    smoothed_once = smooth_inner(plain_rim(scalar_field))
    smoothed = smooth_inner(plain_rim(smoothed_once))
    margined = extended_2(smoothed, (("bx", 1), ("by", 2)), 1)
    padded = jnp.pad(margined, ((1, 1), (0, 0), (0, 0)))
    planes = 8
    step_x = 2.0 / full_x
    step_y = 2.0 / full_y
    upper_x = upper_ones(planes)
    upper_y = upper_ones(local_y)

    def advance(carried, index):
        colour, optical = carried
        window = lax.dynamic_slice_in_dim(padded, index * planes, planes + 2, 1)
        emission, absorption = transfer(window, transfer_in, transfer_out, bands)
        thickness = absorption * step_x
        running = jnp.einsum("bzxy,xw->bzwy", thickness, upper_x, precision=lax.Precision.HIGHEST)
        visible = jnp.exp(-(optical[:, :, None, :] + running - thickness))
        colour = colour + jnp.sum(visible * -jnp.expm1(-thickness) * emission, axis=2)
        optical = optical + running[:, :, -1, :]
        thickness_y = absorption * step_y
        running_y = jnp.einsum(
            "bzxy,yw->bzxw", thickness_y, upper_y, precision=lax.Precision.HIGHEST
        )
        colour_y = jnp.sum(
            jnp.exp(-(running_y - thickness_y)) * -jnp.expm1(-thickness_y) * emission, axis=3
        )
        clear_y = jnp.exp(-running_y[..., -1])
        return ((colour, optical), jnp.stack([colour_y, clear_y]))

    blank = jnp.zeros((bands, layers, local_y), jnp.float32)
    (colour, optical), images = lax.scan(
        advance, (blank, blank), jnp.arange(local_x // planes, dtype=jnp.int32)
    )
    clear_x = jnp.exp(-optical)
    image_y = jnp.transpose(images, (1, 2, 3, 0, 4)).reshape(2, bands, layers, local_x)
    pieces_y = lax.all_to_all(image_y[None], "by", split_axis=3, concat_axis=0, tiled=True)
    view_y = fold_bricks(pieces_y)
    opaque = jnp.ones_like(blank)
    ahead_image = entering((colour, clear_x), "bx", composite, (blank, opaque), False)
    behind = entering((colour, clear_x), "bx", composite_back, (blank, opaque), True)
    combined = composite(composite(ahead_image, (colour, clear_x)), behind)
    slab_x = layers // count_x
    view_x = lax.dynamic_slice_in_dim(
        jnp.stack([combined[0], combined[1]]), lax.axis_index("bx") * slab_x, slab_x, 2
    )
    return (view_x, view_y)


def solution(mesh):
    return jax.shard_map(
        body,
        mesh=mesh,
        in_specs=(P(None, "bx", "by"), P(), P()),
        out_specs=(P(None, None, "bx", "by"), P(None, None, "by", "bx")),
        check_vma=False,
    )
```

profile of v0, /device:TPU:1, one launch (start us, length us, event | category | flops | bytes accessed | tf_op | source)
XLA Modules:
  0.0 570.0 jit_solution(6825985464397569143)
XLA Ops:
  10.4 4.6 collective-permute-start.1
  16.3 5.7 collective-permute-start.2
  25.1 4.2 fusion.47
  30.6 4.6 collective-permute-start.5
  36.6 2.9 collective-permute-start.6
  39.5 3.8 collective-permute-start.7
  44.1 4.2 fusion.40
  48.3 4.0 collective-permute-start.8
  53.6 4.0 collective-permute-done.9
  57.7 5.4 collective-permute-start.10
  65.0 3.1 collective-permute-done.11
  68.1 2.4 select_maximum_fusion
  70.5 243.1 %while.46 = (s32[]{:T(128)}, f32[8,64,128]{2,0,1:T(8,128)}, f32[8,64,128]{2,0,1:T(8,128)}, f32[4,2,8,64,8]{3,4,0,2,1:T(8,128)}, s32[4]{0:T(128)S(1)}, /*index=5*...) while((s32[]{:T(128)}, f32[8,64,128]{2,0,1:T(8,128)}, ...), condition=%wide.region_3.4_spmd.clone, body=%wide.region_0.3_spmd.clone.sunk | while | flops 931544000 | bytes 93905320 | solution.py:165
  76.2 2.9 copy.302
  79.1 2.9 copy.303
  81.9 2.7 sub.69
  88.1 2.3 copy.305
  94.0 3.3 fusion.84
  99.1 3.2 stack.111
  102.3 3.8 convolution_bitcast_fusion.2
  106.1 2.7 fusion.85
  111.0 2.5 copy.315
  116.5 7.3 %fusion.89 = (f32[8,64,8]{0,2,1:T(8,128)S(1)}, f32[8,64,128]{2,0,1:T(8,128)S(1)}) fusion(f32[8,64,8,128]{3,2,1,0:T(8,128)S(1)} %fusion.86, f32[16,64,8,128]{3,0,2,1:T(8,128)} %convolution_bitcast_fusion.2, f32[8,64,128,8]{2,3,1,0:T(8,128)S(1)} %copy-done.1, f32[8,64,128]{2,0,1:T(8,128)S(1)} %get-tuple-element.582), kind=kLoop, calls=%fused_computation.23.clone.1 | loop fusion | flops 13561856 | bytes 8929280 | tf_op jit(solution)/shard_map/while/body/eval_jaxpr/reduce_sum | solution.py:158
  123.9 3.6 slice.461
  127.6 2.4 copy.316
  136.9 2.9 copy.302
  139.8 2.9 copy.303
  142.7 2.7 sub.69
  148.8 2.3 copy.305
  154.7 3.3 fusion.84
  159.8 3.2 stack.111
  163.0 3.8 convolution_bitcast_fusion.2
  166.8 2.7 fusion.85
  171.7 2.5 copy.315
  177.2 7.3 %fusion.89 = (f32[8,64,8]{0,2,1:T(8,128)S(1)}, f32[8,64,128]{2,0,1:T(8,128)S(1)}) fusion(f32[8,64,8,128]{3,2,1,0:T(8,128)S(1)} %fusion.86, f32[16,64,8,128]{3,0,2,1:T(8,128)} %convolution_bitcast_fusion.2, f32[8,64,128,8]{2,3,1,0:T(8,128)S(1)} %copy-done.1, f32[8,64,128]{2,0,1:T(8,128)S(1)} %get-tuple-element.582), kind=kLoop, calls=%fused_computation.23.clone.1 | loop fusion | flops 13561856 | bytes 8929280 | tf_op jit(solution)/shard_map/while/body/eval_jaxpr/reduce_sum | solution.py:158
  184.7 3.6 slice.461
  188.3 2.4 copy.316
  197.6 2.9 copy.302
  200.5 2.9 copy.303
  203.4 2.7 sub.69
  215.4 3.3 fusion.84
  220.5 3.2 stack.111
  223.8 3.8 convolution_bitcast_fusion.2
  227.5 2.7 fusion.85
  232.4 2.5 copy.315
  237.9 7.3 %fusion.89 = (f32[8,64,8]{0,2,1:T(8,128)S(1)}, f32[8,64,128]{2,0,1:T(8,128)S(1)}) fusion(f32[8,64,8,128]{3,2,1,0:T(8,128)S(1)} %fusion.86, f32[16,64,8,128]{3,0,2,1:T(8,128)} %convolution_bitcast_fusion.2, f32[8,64,128,8]{2,3,1,0:T(8,128)S(1)} %copy-done.1, f32[8,64,128]{2,0,1:T(8,128)S(1)} %get-tuple-element.582), kind=kLoop, calls=%fused_computation.23.clone.1 | loop fusion | flops 13561856 | bytes 8929280 | tf_op jit(solution)/shard_map/while/body/eval_jaxpr/reduce_sum | solution.py:158
  245.4 3.6 slice.461
  249.0 2.4 copy.316
  258.3 2.9 copy.302
  261.2 2.9 copy.303
  264.1 2.7 sub.69
  276.1 3.3 fusion.84
  281.2 3.2 stack.111
  284.5 3.8 convolution_bitcast_fusion.2
  288.3 2.7 fusion.85
  293.1 2.5 copy.315
  298.7 7.3 %fusion.89 = (f32[8,64,8]{0,2,1:T(8,128)S(1)}, f32[8,64,128]{2,0,1:T(8,128)S(1)}) fusion(f32[8,64,8,128]{3,2,1,0:T(8,128)S(1)} %fusion.86, f32[16,64,8,128]{3,0,2,1:T(8,128)} %convolution_bitcast_fusion.2, f32[8,64,128,8]{2,3,1,0:T(8,128)S(1)} %copy-done.1, f32[8,64,128]{2,0,1:T(8,128)S(1)} %get-tuple-element.582), kind=kLoop, calls=%fused_computation.23.clone.1 | loop fusion | flops 13561856 | bytes 8929280 | tf_op jit(solution)/shard_map/while/body/eval_jaxpr/reduce_sum | solution.py:158
  306.1 3.6 slice.461
  309.7 2.4 copy.316
  319.2 3.7 all-to-all-start
  323.0 5.3 all-to-all-done
  331.1 94.3 %all-gather.5.cloned.1.call-done = f32[256,64,128]{2,1,0:T(8,128)} async-done(((f32[8,64,128]{2,1,0:T(8,128)}), f32[256,64,128]{2,1,0:T(8,128)}) %all-gather.5.cloned.1.call-update) | async-done | bytes 8388624 | tf_op jit(solution)/shard_map/all_gather | solution.py:24
  425.4 98.0 %all-gather.7.cloned.1.call-done = f32[256,64,128]{2,1,0:T(8,128)} async-done(((f32[8,64,128]{2,1,0:T(8,128)}), f32[256,64,128]{2,1,0:T(8,128)}) %all-gather.7.cloned.1.call-update) | async-done | bytes 8388624 | tf_op jit(solution)/shard_map/all_gather | solution.py:24
  523.6 38.7 %while.45 = (s32[]{:T(128)}, f32[8,64,128]{2,1,0:T(8,128)S(1)}, f32[8,64,128]{2,1,0:T(8,128)S(1)}, s32[]{:T(128)}, f32[32,8,64,128]{3,2,1,0:T(8,128)}, /*index=5...) while((s32[]{:T(128)}, f32[8,64,128]{2,1,0:T(8,128)S(1)}, ...), condition=%wide.region_7.8_spmd, body=%wide.region_6.7_spmd.sunk | while | flops 196614 | bytes 1573015 | solution.py:33
  (273 shorter events, 146.5 us)
Async XLA Ops:
  7.2 418.3 %all-gather.5.cloned.1.call-start = ((), (), s32[]{:S(2)}) async-start(), calls=%async_computation.1 | async-start | bytes 8650752 | tf_op jit(solution)/shard_map/all_gather | solution.py:24
  9.1 5.9 %collective-permute-start = (f32[64,1,128]{0,2,1:T(8,128)S(1)}, f32[64,1,128]{0,2,1:T(8,128)S(1)}, u32[]{:S(2)}, u32[]{:S(2)}) collective-permute-start(f32[64,1,128]{0,2,1:T(8,128)S(1)} %get-tuple-element.408), channel_id=1, source_target_pairs={{8,0},{16,8},{24,16},{32,24},{40,32},{48,40},{56,48},{64,56},{72,6... | collective-permute-start | bytes 98312 | tf_op jit(solution)/shard_map/ppermute | solution.py:15
  10.4 5.9 %collective-permute-start.1 = (f32[64,1,128]{0,2,1:T(8,128)S(1)}, f32[64,1,128]{0,2,1:T(8,128)S(1)}, u32[]{:S(2)}, u32[]{:S(2)}) collective-permute-start(f32[64,1,128]{0,2,1:T(8,128)S(1)} %get-tuple-element.407), channel_id=1, source_target_pairs={{0,8},{8,16},{16,24},{24,32},{32,40},{40,48},{48,56},{56,64},{64,7... | collective-permute-start | bytes 98312 | tf_op jit(solution)/shard_map/ppermute | solution.py:14
  16.3 7.6 %collective-permute-start.2 = (f32[64,34,1]{0,2,1:T(1,128)S(1)}, f32[64,34,1]{0,2,1:T(1,128)S(1)}, u32[]{:S(2)}, u32[]{:S(2)}) collective-permute-start(f32[64,34,1]{0,2,1:T(1,128)S(1)} %get-tuple-element.401), channel_id=1, source_target_pairs={{1,0},{2,1},{3,2},{4,3},{5,4},{6,5},{7,6},{9,8},{10,9},{11,10},{12... | collective-permute-start | bytes 26120 | tf_op jit(solution)/shard_map/ppermute | solution.py:15
  22.0 3.1 collective-permute-start.3
  29.3 6.3 %collective-permute-start.4 = (f32[64,1,128]{0,2,1:T(8,128)S(1)}, f32[64,1,128]{0,2,1:T(8,128)S(1)}, u32[]{:S(2)}, u32[]{:S(2)}) collective-permute-start(f32[64,1,128]{0,2,1:T(8,128)S(1)} %get-tuple-element.406), channel_id=1, source_target_pairs={{8,0},{16,8},{24,16},{32,24},{40,32},{48,40},{56,48},{64,56},{72,6... | collective-permute-start | bytes 98312 | tf_op jit(solution)/shard_map/ppermute | solution.py:15
  30.6 5.9 %collective-permute-start.5 = (f32[64,1,128]{0,2,1:T(8,128)S(1)}, f32[64,1,128]{0,2,1:T(8,128)S(1)}, u32[]{:S(2)}, u32[]{:S(2)}) collective-permute-start(f32[64,1,128]{0,2,1:T(8,128)S(1)} %get-tuple-element.405), channel_id=1, source_target_pairs={{0,8},{8,16},{16,24},{24,32},{32,40},{40,48},{48,56},{56,64},{64,7... | collective-permute-start | bytes 98312 | tf_op jit(solution)/shard_map/ppermute | solution.py:14
  36.6 6.7 %collective-permute-start.6 = (f32[64,34,1]{0,2,1:T(1,128)S(1)}, f32[64,34,1]{0,2,1:T(1,128)S(1)}, u32[]{:S(2)}, u32[]{:S(2)}) collective-permute-start(f32[64,34,1]{0,2,1:T(1,128)S(1)} %get-tuple-element.399), channel_id=1, source_target_pairs={{1,0},{2,1},{3,2},{4,3},{5,4},{6,5},{7,6},{9,8},{10,9},{11,10},{12... | collective-permute-start | bytes 26120 | tf_op jit(solution)/shard_map/ppermute | solution.py:15
  39.5 4.6 collective-permute-start.7
  48.3 9.3 %copy-start.5 = (f32[64,32,128]{0,2,1:T(8,128)}, f32[64,32,128]{0,2,1:T(8,128)S(1)}, u32[]{:S(2)}) copy-start(f32[64,32,128]{0,2,1:T(8,128)S(1)} %fusion.40) | copy-start | bytes 3145732
  48.3 5.3 collective-permute-start.8
  52.3 5.3 collective-permute-start.9
  57.7 7.3 %collective-permute-start.10 = (f32[64,34,1]{0,2,1:T(1,128)S(1)}, f32[64,34,1]{0,2,1:T(1,128)S(1)}, u32[]{:S(2)}, u32[]{:S(2)}) collective-permute-start(f32[64,34,1]{0,2,1:T(1,128)S(1)} %get-tuple-element.397), channel_id=1, source_target_pairs={{0,1},{1,2},{2,3},{3,4},{4,5},{5,6},{6,7},{8,9},{9,10},{10,11},{11... | collective-permute-start | bytes 26120 | tf_op jit(solution)/shard_map/ppermute | solution.py:14
  63.0 5.1 collective-permute-start.11
  65.0 5.5 copy-start.12
  65.0 5.5 copy-start.13
  70.7 21.0 %copy-start.3 = (f32[66,34,130]{0,2,1:T(8,128)}, f32[66,34,130]{0,2,1:T(8,128)S(1)}, u32[]{:S(2)}) copy-start(f32[66,34,130]{0,2,1:T(8,128)S(1)} %get-tuple-element.621) | copy-start | bytes 3500644 | tf_op jit(solution)/shard_map/while
  111.0 2.6 copy-start
  111.0 2.6 copy-start.9
  114.6 1.9 copy-start.10
  114.6 1.9 copy-start.1
  116.5 7.3 %copy-start.2 = (f32[8,64,8,128]{3,2,1,0:T(8,128)}, f32[8,64,8,128]{3,2,1,0:T(8,128)S(1)}, u32[]{:S(2)}) copy-start(f32[8,64,8,128]{3,2,1,0:T(8,128)S(1)} %fusion.86) | copy-start | bytes 6291460 | tf_op jit(solution)/shard_map/while
  123.9 6.7 %copy-start.6 = (f32[8,64,128]{2,0,1:T(8,128)S(1)}, f32[8,64,128]{2,0,1:T(8,128)}, u32[]{:S(2)}) copy-start(f32[8,64,128]{2,0,1:T(8,128)} %get-tuple-element.602) | copy-start | bytes 786436 | tf_op jit(solution)/shard_map/while
  127.6 3.9 copy-start.4
  130.7 0.7 copy-start.7
  131.4 21.0 %copy-start.3 = (f32[66,34,130]{0,2,1:T(8,128)}, f32[66,34,130]{0,2,1:T(8,128)S(1)}, u32[]{:S(2)}) copy-start(f32[66,34,130]{0,2,1:T(8,128)S(1)} %get-tuple-element.621) | copy-start | bytes 3500644 | tf_op jit(solution)/shard_map/while
  171.7 2.6 copy-start
  171.7 2.6 copy-start.9
  175.3 1.9 copy-start.10
  175.3 1.9 copy-start.1
  177.2 7.3 %copy-start.2 = (f32[8,64,8,128]{3,2,1,0:T(8,128)}, f32[8,64,8,128]{3,2,1,0:T(8,128)S(1)}, u32[]{:S(2)}) copy-start(f32[8,64,8,128]{3,2,1,0:T(8,128)S(1)} %fusion.86) | copy-start | bytes 6291460 | tf_op jit(solution)/shard_map/while
  184.7 6.7 %copy-start.6 = (f32[8,64,128]{2,0,1:T(8,128)S(1)}, f32[8,64,128]{2,0,1:T(8,128)}, u32[]{:S(2)}) copy-start(f32[8,64,128]{2,0,1:T(8,128)} %get-tuple-element.602) | copy-start | bytes 786436 | tf_op jit(solution)/shard_map/while
  188.3 3.9 copy-start.4
  191.5 0.7 copy-start.7
  192.2 21.0 %copy-start.3 = (f32[66,34,130]{0,2,1:T(8,128)}, f32[66,34,130]{0,2,1:T(8,128)S(1)}, u32[]{:S(2)}) copy-start(f32[66,34,130]{0,2,1:T(8,128)S(1)} %get-tuple-element.621) | copy-start | bytes 3500644 | tf_op jit(solution)/shard_map/while
  232.4 2.6 copy-start
  232.4 2.6 copy-start.9
  236.0 1.9 copy-start.10
  236.0 1.9 copy-start.1
  237.9 7.3 %copy-start.2 = (f32[8,64,8,128]{3,2,1,0:T(8,128)}, f32[8,64,8,128]{3,2,1,0:T(8,128)S(1)}, u32[]{:S(2)}) copy-start(f32[8,64,8,128]{3,2,1,0:T(8,128)S(1)} %fusion.86) | copy-start | bytes 6291460 | tf_op jit(solution)/shard_map/while
  245.4 6.7 %copy-start.6 = (f32[8,64,128]{2,0,1:T(8,128)S(1)}, f32[8,64,128]{2,0,1:T(8,128)}, u32[]{:S(2)}) copy-start(f32[8,64,128]{2,0,1:T(8,128)} %get-tuple-element.602) | copy-start | bytes 786436 | tf_op jit(solution)/shard_map/while
  249.0 3.9 copy-start.4
  252.2 0.7 copy-start.7
  252.9 21.0 %copy-start.3 = (f32[66,34,130]{0,2,1:T(8,128)}, f32[66,34,130]{0,2,1:T(8,128)S(1)}, u32[]{:S(2)}) copy-start(f32[66,34,130]{0,2,1:T(8,128)S(1)} %get-tuple-element.621) | copy-start | bytes 3500644 | tf_op jit(solution)/shard_map/while
  293.1 2.6 copy-start
  293.1 2.6 copy-start.9
  296.7 1.9 copy-start.10
  296.7 1.9 copy-start.1
  298.6 7.3 %copy-start.2 = (f32[8,64,8,128]{3,2,1,0:T(8,128)}, f32[8,64,8,128]{3,2,1,0:T(8,128)S(1)}, u32[]{:S(2)}) copy-start(f32[8,64,8,128]{3,2,1,0:T(8,128)S(1)} %fusion.86) | copy-start | bytes 6291460 | tf_op jit(solution)/shard_map/while
  306.1 6.7 %copy-start.6 = (f32[8,64,128]{2,0,1:T(8,128)S(1)}, f32[8,64,128]{2,0,1:T(8,128)}, u32[]{:S(2)}) copy-start(f32[8,64,128]{2,0,1:T(8,128)} %get-tuple-element.602) | copy-start | bytes 786436 | tf_op jit(solution)/shard_map/while
  309.7 3.9 copy-start.4
  312.9 0.7 copy-start.7
  315.3 208.1 %all-gather.7.cloned.1.call-start = ((), (), s32[]{:S(2)}) async-start(), calls=%async_computation.2 | async-start | bytes 8650752 | tf_op jit(solution)/shard_map/all_gather | solution.py:24
  319.2 9.0 %all-to-all-start = ((f32[8,1,4096]{2,1,0:T(1,128)}), f32[8,1,4096]{2,1,0:T(1,128)S(1)}, u32[]{:S(2)}, u32[]{:S(2)}) async-start(f32[8,1,4096]{2,1,0:T(1,128)} %reshape.36), calls=%async_computation | async-start | bytes 262144 | tf_op jit(solution)/shard_map/all_to_all | solution.py:170
  523.6 38.8 %copy-start.8 = (f32[8,64,128]{2,0,1:T(8,128)S(1)}, f32[8,64,128]{2,0,1:T(8,128)}, u32[]{:S(2)}) copy-start(f32[8,64,128]{2,0,1:T(8,128)} %get-tuple-element.271) | copy-start | bytes 786436
  523.6 38.8 %copy-start.11 = (f32[8,64,128]{2,0,1:T(8,128)S(1)}, f32[8,64,128]{2,0,1:T(8,128)}, u32[]{:S(2)}) copy-start(f32[8,64,128]{2,0,1:T(8,128)} %get-tuple-element.272) | copy-start | bytes 786436
Sparse Core Ops, SparseCore 0:
  315.4 109.9 all-gather.4
  428.0 95.4 all-gather.6
where the time goes:
time: 573 us; the launch traced here: 570 us
  waiting for transfers between devices  209 us (36%)
  other arithmetic  135 us (24%)
  local copies, waits for them, and re-layouts  133 us (23%)
  starting transfers between devices  42.4 us (7%)
  matrix products  31.1 us (5%)
  between operations  14.4 us (3%)
    all_gather x2, waiting for transfers between devices, entering(): gathered = jax.tree.map(lambda a: lax.all_gather(a, axis), part)  192 us
    while x104, local copies, waits for them, and re-layouts  65.1 us
    mul x31, other arithmetic, composite(): ahead_pair[1] * later_pair[1]  37.9 us
    reduce_sum x4, other arithmetic, advance(): jnp.sum(jnp.exp(-(running_y - thickness_y)) * -jnp.expm1(-thickness_y) *...  29.2 us
    ppermute x6, starting transfers between devices, extended_2(): before = lax.ppermute(last, axis, up)  24.2 us
    another operation x32, local copies, waits for them, and re-layouts, transfer(): jnp.stack([centre, scaled_x, scaled_y, scaled_z, magnitude, centre * magn...  18.7 us
    dot_general x4, matrix products, transfer(): jnp.einsum('ch,hzxy->czxy', transfer_out, hidden, preferred_element_type=...  15.1 us
    slice x4, local copies, waits for them, and re-layouts, advance(): clear_y = jnp.exp(-running_y[..., -1])  14.5 us
  transfers between devices with their start and end apart: 15, of which 10 were waited for; matrix products, arithmetic and copies ran while one was open for 1% of the time, Pallas kernels for 0%

commit v1 on v0

v1 whole, which is shorter than its diff:
```python
import jax
import jax.numpy as jnp
from jax import lax
from jax.experimental import pallas as pl
from jax.experimental.pallas import tpu as pltpu
from jax.sharding import PartitionSpec as P

BANDS = 8
HID = 16
FEAT = 8
LOG2E = 1.4426950408889634
GROUP = 4


def extended(shard, sides, width):
    for axis, dim in sides:
        peers, length = (lax.axis_size(axis), shard.shape[dim])
        up = [(i, i + 1) for i in range(peers - 1)]
        down = [(j, i) for i, j in up]
        last = lax.slice_in_dim(shard, length - width, length, axis=dim)
        initial = lax.slice_in_dim(shard, 0, width, axis=dim)
        before = lax.ppermute(last, axis, up)
        after = lax.ppermute(initial, axis, down)
        shard = jnp.concatenate([before, shard, after], axis=dim)
    return shard


def lanes_of():
    return lax.broadcasted_iota(jnp.int32, (8, 128), 1)


def softplus(v):
    grown = jnp.exp2(jnp.minimum(v * LOG2E, 126.0))
    return jnp.maximum(v, jnp.log(1.0 + grown))


def render(place_ref, tb_ref, w1_ref, w2_ref, j_ref, r_ref, s1_ref, p_ref, b_ref, d_ref, x_ref, yc_ref, yt_ref, rs_ref):
    lane = lanes_of()
    seg = lax.broadcasted_iota(jnp.int32, (8, 128), 0)
    z = lane & 63
    half = lane >> 6
    top = z == 0
    bottom = z == 63
    full_x = place_ref[2]
    full_y = place_ref[3]
    at_x = place_ref[0] * 32 + half * 16
    at_y = place_ref[1] * 128 + seg * 16

    def above(v):
        return jnp.where(top, 0.0, pltpu.roll(v, 1, 1))

    def below(v):
        return jnp.where(bottom, 0.0, pltpu.roll(v, 127, 1))

    def in_x(xp):
        g = at_x + xp
        return (g >= 0) & (g < full_x)

    def in_y(yp):
        g = at_y + yp
        return (g >= 0) & (g < full_y)

    def first(i, carry):
        mine = in_x(i - 2)
        mid = [tb_ref[i + 1, pl.ds(k, 8, stride=16), :] for k in range(22)]
        for k in range(20):
            c = mid[k + 1]
            near = tb_ref[i, pl.ds(k + 1, 8, stride=16), :] + tb_ref[i + 2, pl.ds(k + 1, 8, stride=16), :]
            near = near + mid[k] + mid[k + 2] + above(c) + below(c)
            ok = mine if 2 <= k < 18 else mine & in_y(k - 2)
            s1_ref[i, k] = jnp.where(ok, 0.4 * c + 0.1 * near, 0.0)
        return carry

    lax.fori_loop(0, 20, first, 0)

    def second(i, carry):
        mine = in_x(i - 1)
        mid = [s1_ref[i + 1, k] for k in range(20)]
        for k in range(18):
            c = mid[k + 1]
            near = s1_ref[i, k + 1] + s1_ref[i + 2, k + 1]
            near = near + mid[k] + mid[k + 2] + above(c) + below(c)
            ok = mine if 1 <= k < 17 else mine & in_y(k - 1)
            s = jnp.where(ok, 0.4 * c + 0.1 * near, 0.0)
            up, down = above(s), below(s)
            p_ref[i, k] = s
            b_ref[i, k] = 2.0 * s + (up + down)
            d_ref[i, k] = down - up
        return carry

    lax.fori_loop(0, 18, second, 0)

    for b in range(BANDS):
        yc_ref[b] = jnp.zeros((128, 128), jnp.float32)
        yt_ref[b] = jnp.ones((128, 128), jnp.float32)

    def features(i, k):
        s = p_ref[i, k]
        a = p_ref[i + 1, k + 1] - p_ref[i - 1, k - 1]
        c = p_ref[i + 1, k - 1] - p_ref[i - 1, k + 1]
        gx = (b_ref[i + 1, k] - b_ref[i - 1, k] + (a + c)) * (1.0 / 3.0)
        gy = (b_ref[i, k + 1] - b_ref[i, k - 1] + (a - c)) * (1.0 / 3.0)
        d = d_ref[i, k]
        gz = (d + d + (d_ref[i + 1, k] + d_ref[i - 1, k]) + (d_ref[i, k + 1] + d_ref[i, k - 1])) * (1.0 / 3.0)
        q = 1.0 + gx * gx + gy * gy + gz * gz
        m = q * lax.rsqrt(q)
        return s, gx, gy, gz, m, s * m, s * s

    one = jnp.ones((8, 128), jnp.float32)
    w1 = w1_ref[...]
    w2 = w2_ref[...]

    def columns(k, carry):
        def cells(g, state):
            state = list(state)
            for n in range(GROUP):
                rows = list(features(g * GROUP + n + 1, k + 1)) + [one]
                for f in range(0, FEAT, 2):
                    pair = jnp.concatenate([rows[f], rows[f + 1]], axis=0)
                    x_ref[8 * f : 8 * f + 16, 128 * n : 128 * n + 128] = pair.astype(jnp.bfloat16)
            u = jnp.dot(w1, x_ref[...], preferred_element_type=jnp.float32)
            hidden = (u + u * jnp.tanh(u)).astype(jnp.bfloat16)
            ch = jnp.dot(w2, hidden, preferred_element_type=jnp.float32)
            for n in range(GROUP):
                row = pl.multiple_of((g * GROUP + n) * 8, 8)
                for b in range(BANDS):
                    e = softplus(ch[8 * b : 8 * b + 8, 128 * n : 128 * n + 128])
                    t = softplus(ch[64 + 8 * b : 72 + 8 * b, 128 * n : 128 * n + 128])
                    q = jnp.exp2(t * (-LOG2E / 512.0))
                    tx = state[8 + b]
                    nx = tx * q
                    state[b] = state[b] + (tx - nx) * e
                    state[8 + b] = nx
                    ty = yt_ref[b, pl.ds(row, 8), :]
                    ny = ty * q
                    yc_ref[b, pl.ds(row, 8), :] = yc_ref[b, pl.ds(row, 8), :] + (ty - ny) * e
                    yt_ref[b, pl.ds(row, 8), :] = ny
            return tuple(state)

        start = (jnp.zeros((8, 128), jnp.float32),) * BANDS + (one,) * BANDS
        state = lax.fori_loop(0, 16 // GROUP, cells, start)
        colour = [state[b] + state[8 + b] * pltpu.roll(state[b], 64, 1) for b in range(BANDS)]
        clear = [state[8 + b] * pltpu.roll(state[8 + b], 64, 1) for b in range(BANDS)]
        image = jnp.transpose(jnp.concatenate(colour + clear, axis=0))
        j_ref[pl.ds(k, 64, stride=16), :] = image[0:64]
        return carry

    lax.fori_loop(0, 16, columns, 0)

    for b in range(BANDS):
        for h in range(2):
            colour = yc_ref[b, pl.ds(64 * h, 8, stride=8), :]
            clear = yt_ref[b, pl.ds(64 * h, 8, stride=8), :]
            for s in range(1, 8):
                colour = colour + clear * yc_ref[b, pl.ds(64 * h + s, 8, stride=8), :]
                clear = clear * yt_ref[b, pl.ds(64 * h + s, 8, stride=8), :]
            rs_ref[0, 16 * b + 8 * h : 16 * b + 8 * h + 8, :] = colour
            rs_ref[1, 16 * b + 8 * h : 16 * b + 8 * h + 8, :] = clear
    for kind in range(2):
        image = jnp.transpose(rs_ref[kind])
        for h in range(2):
            for p in range(8):
                r_ref[p, h, :, 128 * kind : 128 * kind + 128] = image[64 * h + 8 * p : 64 * h + 8 * p + 8]


def render_call(place, tb, w1, w2):
    vmem = pl.BlockSpec(memory_space=pltpu.VMEM)
    return pl.pallas_call(
        render,
        out_shape=(
            jax.ShapeDtypeStruct((1024, 128), jnp.float32),
            jax.ShapeDtypeStruct((8, 2, 8, 256), jnp.float32),
        ),
        in_specs=[pl.BlockSpec(memory_space=pltpu.SMEM), vmem, vmem, vmem],
        out_specs=(vmem, vmem),
        scratch_shapes=[
            pltpu.VMEM((20, 20, 8, 128), jnp.float32),
            pltpu.VMEM((18, 18, 8, 128), jnp.float32),
            pltpu.VMEM((18, 18, 8, 128), jnp.float32),
            pltpu.VMEM((18, 18, 8, 128), jnp.float32),
            pltpu.VMEM((64, 128 * GROUP), jnp.bfloat16),
            pltpu.VMEM((8, 128, 128), jnp.float32),
            pltpu.VMEM((8, 128, 128), jnp.float32),
            pltpu.VMEM((2, 128, 128), jnp.float32),
        ],
        compiler_params=pltpu.CompilerParams(vmem_limit_bytes=40 << 20),
        name="render",
    )(place, tb, w1, w2)


def fold(jr_ref, rr_ref, vx_ref, vy_ref, at_ref):
    count_x = jr_ref.shape[0]
    count_y = rr_ref.shape[0]
    lane = lax.broadcasted_iota(jnp.int32, (32, 128), 1)
    low = lane < 64

    def over(s, pair):
        front, clear = pair
        piece = jr_ref[s]
        both = jnp.where(low, pltpu.roll(piece, 64, 1), piece)
        return jnp.where(low, front, 0.0) + clear * piece, clear * both

    start = (jnp.zeros((32, 128), jnp.float32), jnp.ones((32, 128), jnp.float32))
    image, _ = lax.fori_loop(0, count_x, over, start)
    at_ref[...] = jnp.zeros_like(at_ref)
    at_ref[0:32, :] = image
    at_ref[...] = jnp.transpose(at_ref[...])
    line = lax.broadcasted_iota(jnp.int32, (16, 128), 1)
    for z in range(2):
        row = jnp.zeros((16, 128), jnp.float32)
        for s in range(8):
            part = at_ref[pl.ds(s, 16, stride=8), :]
            shift = (16 * s - 16 * z) % 128
            part = pltpu.roll(part, shift, 1) if shift else part
            row = jnp.where((line >> 4) == s, part, row)
        vx_ref[:, z, :] = row

    def over_y(s, pair):
        piece = rr_ref[s]
        return pair[0] + pair[1] * piece[:, 0:128], pair[1] * piece[:, 128:256]

    start = (jnp.zeros((16, 128), jnp.float32), jnp.ones((16, 128), jnp.float32))
    kinds = lax.fori_loop(0, count_y, over_y, start)
    lane8 = lanes_of()
    for kind in range(2):
        for b in range(BANDS):
            shift = (128 - 16 * b) % 128
            front = kinds[kind][0:8]
            back = kinds[kind][8:16]
            front = pltpu.roll(front, shift, 1) if shift else front
            back = pltpu.roll(back, shift + 16, 1) if shift < 112 else back
            vy_ref[8 * kind + b] = jnp.where(lane8 < 16, front, back)[:, 0:32]


def fold_call(jr, rr):
    vmem = pl.BlockSpec(memory_space=pltpu.VMEM)
    return pl.pallas_call(
        fold,
        out_shape=(
            jax.ShapeDtypeStruct((16, 2, 128), jnp.float32),
            jax.ShapeDtypeStruct((16, 8, 32), jnp.float32),
        ),
        in_specs=[vmem, vmem],
        out_specs=(vmem, vmem),
        scratch_shapes=[pltpu.VMEM((128, 128), jnp.float32)],
        name="fold",
    )(jr, rr)


def spread(weights, scale):
    rows, cols = weights.shape
    eye = jnp.eye(8, dtype=jnp.float32)
    big = (weights.astype(jnp.float32) * scale)[:, None, :, None] * eye[None, :, None, :]
    return big.reshape(rows * 8, cols * 8).astype(jnp.bfloat16)


def body(scalar_field, transfer_in, transfer_out):
    count_x = lax.axis_size("bx")
    count_y = lax.axis_size("by")
    wide = extended(scalar_field, (("bx", 1), ("by", 2)), 3)
    wide = jnp.pad(wide, ((0, 0), (0, 0), (0, 2)))
    halves = jnp.stack([wide[:, 0:22], wide[:, 16:38]])
    tb = jnp.transpose(halves, (2, 3, 0, 1)).reshape(22, 136, 128)
    place = jnp.stack(
        [lax.axis_index("bx"), lax.axis_index("by"), jnp.int32(32 * count_x), jnp.int32(128 * count_y)]
    ).astype(jnp.int32)
    j, r = render_call(place, tb, spread(transfer_in, 0.5), spread(transfer_out, 1.0))
    slab = 64 // count_x
    jr = lax.all_to_all(j.reshape(count_x, slab * 16, 128), "bx", split_axis=0, concat_axis=0, tiled=True)
    rr = lax.all_to_all(r.reshape(count_y, 128 // count_y, 256), "by", split_axis=0, concat_axis=0, tiled=True)
    vx, vy = fold_call(jr, rr)
    return (vx.reshape(2, 8, slab, 128), vy.reshape(2, 8, 8, 32))


def solution(mesh):
    return jax.shard_map(
        body,
        mesh=mesh,
        in_specs=(P(None, "bx", "by"), P(), P()),
        out_specs=(P(None, None, "bx", "by"), P(None, None, "by", "bx")),
        check_vma=False,
    )
```

time: 573 us -> 121 us (0.21)
  waiting for transfers between devices: 209 us -> 9.98 us
  other arithmetic: 135 us -> 2.59 us
  local copies, waits for them, and re-layouts: 133 us -> 12.4 us
  Pallas kernels: 0 us -> 43.3 us
  blocking collectives: 0 us -> 37.9 us
  matrix products: 31.1 us -> 0 us
  starting transfers between devices: 42.4 us -> 12.1 us
  between operations: 14.4 us -> 0.8 us
    all_gather x2 -> x0, waiting for transfers between devices: 192 us -> none  [entering(): gathered = jax.tree.map(lambda a: lax.all_gather(a, axis), part)]
    while x105 -> x0, local copies, waits for them, and re-layouts: 66.8 us -> none
    mul x36 -> x1, other arithmetic: 48.9 us -> 0.01 us  [spread(): weights.astype(jnp.float32) * scale]
    pallas_call x0 -> x2, Pallas kernels: none -> 43.3 us  [the longest x1 39 us: render_call(): pl.pallas_call(render, out_shape=(jax.ShapeDtypeStruct((1024, 128), jnp.f...]
    all_to_all x0 -> x2, blocking collectives: none -> 37.9 us  [the longest x1 28.4 us: body(): lax.all_to_all(j.reshape(count_x, slab * 16, 128), 'bx', split_axis=0, co...]
    dot_general x12 -> x0, matrix products: 31.1 us -> none  [the longest x4 15.1 us: transfer(): jnp.einsum('ch,hzxy->czxy', transfer_out, hidden, preferred_element_type=...]
    reduce_sum x4 -> x0, other arithmetic: 29.2 us -> none  [advance(): jnp.sum(jnp.exp(-(running_y - thickness_y)) * -jnp.expm1(-thickness_y) *...]
    slice x25 -> x1, local copies, waits for them, and re-layouts: 28.9 us -> 0.89 us  [extended(): last = lax.slice_in_dim(shard, length - width, length, axis=dim)]
  transfers between devices with their start and end apart: 15 -> 4, of which waited for: 10 -> 3; matrix products, arithmetic and copies ran while one was open for 1% -> 1% of each run, Pallas kernels for 0% -> 0%
where the time goes in v1:
time: 121 us; the launch traced here: 119 us
  Pallas kernels  43.3 us (36%)
  blocking collectives  37.9 us (31%)
  local copies, waits for them, and re-layouts  12.4 us (10%)
  starting transfers between devices  12.1 us (10%)
  waiting for transfers between devices  9.98 us (8%)
  other arithmetic  2.59 us (2%)
    pallas_call x1, Pallas kernels, render_call(): pl.pallas_call(render, out_shape=(jax.ShapeDtypeStruct((1024, 128), jnp.f...  39 us
    all_to_all x1, blocking collectives, body(): lax.all_to_all(j.reshape(count_x, slab * 16, 128), 'bx', split_axis=0, co...  28.4 us
    all_to_all x1, blocking collectives, body(): lax.all_to_all(r.reshape(count_y, 128 // count_y, 256), 'by', split_axis=...  9.47 us
    ppermute x2, starting transfers between devices, extended(): before = lax.ppermute(last, axis, up)  8.89 us
    ppermute x2, waiting for transfers between devices, extended(): after = lax.ppermute(initial, axis, down)  6.42 us
    pallas_call x1, Pallas kernels, fold_call(): pl.pallas_call(fold, out_shape=(jax.ShapeDtypeStruct((16, 2, 128), jnp.fl...  4.29 us
    transpose x1, local copies, waits for them, and re-layouts, body(): tb = jnp.transpose(halves, (2, 3, 0, 1)).reshape(22, 136, 128)  3.99 us
    ppermute x2, waiting for transfers between devices, extended(): before = lax.ppermute(last, axis, up)  3.55 us
  transfers between devices with their start and end apart: 4, of which 3 were waited for; matrix products, arithmetic and copies ran while one was open for 1% of the time, Pallas kernels for 0%

profile of v1, /device:TPU:1, one launch (start us, length us, event | category | flops | bytes accessed | tf_op | source)
XLA Modules:
  0.0 119.0 jit_solution(4692703268372940072)
XLA Ops:
  0.6 0.0 copy-start
  0.6 0.0 copy-start.1
  0.6 3.0 %copy.26 = f32[64,32,128]{0,1,2:T(8,128)S(1)} copy(f32[64,32,128]{2,1,0:T(8,128)} %param.3) | data formatting | bytes 2097152 | tf_op args[0]
  3.7 0.9 fusion.6
  4.6 3.9 %collective-permute-start = (f32[64,3,128]{0,1,2:T(4,128)}, f32[64,3,128]{0,1,2:T(4,128)S(1)}, u32[]{:S(2)}, u32[]{:S(2)}) collective-permute-start(f32[64,3,128]{0,1,2:T(4,128)} %get-tuple-element.14), channel_id=1, source_target_pairs={{0,8},{8,16},{16,24},{24,32},{32,40},{40,48},{48,56},{56,64},{64,7... | collective-permute-start | bytes 294920 | tf_op jit(solution)/shard_map/ppermute | solution.py:22
  8.5 1.3 %collective-permute-start.1 = (f32[64,3,128]{0,1,2:T(4,128)}, f32[64,3,128]{0,1,2:T(4,128)S(1)}, u32[]{:S(2)}, u32[]{:S(2)}) collective-permute-start(f32[64,3,128]{0,1,2:T(4,128)} %get-tuple-element.15), channel_id=1, source_target_pairs={{8,0},{16,8},{24,16},{32,24},{40,32},{48,40},{56,48},{64,56},{72,6... | collective-permute-start | bytes 294920 | tf_op jit(solution)/shard_map/ppermute | solution.py:23
  9.9 0.0 copy-done
  9.9 0.1 copy.30
  9.9 0.1 multiply_convert_fusion
  10.1 0.0 copy-done.1
  10.1 0.1 multiply_convert_fusion.1
  10.2 3.6 %collective-permute-done = f32[64,3,128]{0,1,2:T(4,128)S(1)} collective-permute-done((f32[64,3,128]{0,1,2:T(4,128)}, f32[64,3,128]{0,1,2:T(4,128)S(1)}, u32[]{:S(2)}, u32[]{:S(2)}) %collective-permute-start) | collective-permute-done | bytes 98336 | tf_op jit(solution)/shard_map/ppermute | solution.py:22
  13.8 3.7 %collective-permute-done.1 = f32[64,3,128]{0,1,2:T(4,128)S(1)} collective-permute-done((f32[64,3,128]{0,1,2:T(4,128)}, f32[64,3,128]{0,1,2:T(4,128)S(1)}, u32[]{:S(2)}, u32[]{:S(2)}) %collective-permute-start.1) | collective-permute-done | bytes 98336 | tf_op jit(solution)/shard_map/ppermute | solution.py:23
  17.5 0.6 pad_maximum_fusion.2
  18.2 4.9 %collective-permute-start.2 = (f32[64,38,3]{0,1,2:T(8,128)}, f32[64,38,3]{0,1,2:T(8,128)}, u32[]{:S(2)}, u32[]{:S(2)}) collective-permute-start(f32[64,38,3]{0,1,2:T(8,128)} %get-tuple-element.12), channel_id=1, source_target_pairs={{0,1},{1,2},{2,3},{3,4},{4,5},{5,6},{6,7},{8,9},{9,10},{10,11},{11... | collective-permute-start | bytes 87560 | tf_op jit(solution)/shard_map/ppermute | solution.py:22
  23.1 1.9 %collective-permute-start.3 = (f32[64,38,3]{0,1,2:T(8,128)S(1)}, f32[64,38,3]{0,1,2:T(8,128)}, u32[]{:S(2)}, u32[]{:S(2)}) collective-permute-start(f32[64,38,3]{0,1,2:T(8,128)S(1)} %get-tuple-element.13), channel_id=1, source_target_pairs={{1,0},{2,1},{3,2},{4,3},{5,4},{6,5},{7,6},{9,8},{10,9},{11,10},{12... | collective-permute-start | bytes 87560 | tf_op jit(solution)/shard_map/ppermute | solution.py:23
  25.0 0.1 pad_add_fusion.place_ref
  25.1 0.5 convert_element_type.34.w2_ref
  25.6 0.2 convert_element_type.31
  25.9 0.1 copy.31.w1_ref
  26.0 0.0 collective-permute-done.2
  26.0 2.7 %collective-permute-done.3 = f32[64,38,3]{0,1,2:T(8,128)} collective-permute-done((f32[64,38,3]{0,1,2:T(8,128)S(1)}, f32[64,38,3]{0,1,2:T(8,128)}, u32[]{:S(2)}, u32[]{:S(2)}) %collective-permute-start.3) | collective-permute-done | bytes 29216 | tf_op jit(solution)/shard_map/ppermute | solution.py:23
  28.8 1.3 %select_maximum_fusion = f32[64,38,136]{0,1,2:T(8,128)S(1)} fusion(f32[64,38,3]{0,1,2:T(8,128)} %collective-permute-done.3, f32[64,38,3]{0,1,2:T(8,128)} %collective-permute-done.2, f32[64,3,128]{0,1,2:T(4,128)S(1)} %collective-permute-done.1, f32[64,32,128]{0,1,2:T(8,128)S(1)} %copy.26, f32[64,3,128]{0,1,2:T(4,128)S(1)} %collective-permute-done), kind=kLoop, calls=%fused_computation.1 | loop fusion | flops 3307520 | bytes 2626560 | tf_op jit(solution)/shard_map/concatenate | solution.py:24
  30.1 0.2 slice_bitcast_fusion.1
  30.3 0.2 maximum_bitcast_fusion
  30.6 4.0 %copy.29 = f32[22,136,2,64]{3,2,1,0:T(2,128)} copy(f32[22,136,2,64]{3,0,1,2:T(8,128)S(1)} %maximum_bitcast_fusion) | data formatting | bytes 3063808 | tf_op jit(solution)/shard_map/transpose | solution.py:263
  34.6 3.3 %reshape.39.tb_ref = f32[22,136,128]{2,1,0:T(8,128)S(1)} reshape(f32[22,136,2,64]{3,2,1,0:T(2,128)} %copy.29) | data formatting | bytes 3063808 | tf_op jit(solution)/shard_map/reshape | solution.py:263
  37.9 39.0 %render.1 = (f32[1024,128]{1,0:T(8,128)S(1)}, f32[8,2,8,256]{3,2,1,0:T(8,128)S(1)}) custom-call(s32[4]{0:T(128)S(1)} %pad_add_fusion.place_ref, f32[22,136,128]{2,1,0:T(8,128)S(1)} %reshape.39.tb_ref, bf16[128,64]{1,0:T(8,128)(2,1)S(1)} %copy.31.w1_ref, bf16[128,128]{1,0:T(8,128)(2,1)S(1)} %convert_element_type.34.w2_ref), custom_call_target="tpu_custom_call" | custom-call | tf_op jit(solution)/shard_map/render/pallas_call | solution.py:168
  76.9 9.5 %all_to_all.10.rr_ref = f32[8,16,256]{2,1,0:T(8,128)} all-to-all(f32[8,16,256]{2,1,0:T(8,128)S(1)} %bitcast.19), channel_id=1, replica_groups=mesh['bx'=32,'by'=8] {'by'}, dimensions={0} | all-to-all | bytes 262144 | tf_op jit(solution)/shard_map/all_to_all | solution.py:270
  86.3 28.4 %all_to_all.11.jr_ref = f32[32,32,128]{2,1,0:T(8,128)} all-to-all(f32[32,32,128]{2,1,0:T(8,128)S(1)} %bitcast.18), channel_id=1, replica_groups=mesh['bx'=32,'by'=8] {'bx'}, dimensions={0} | all-to-all | bytes 1048576 | tf_op jit(solution)/shard_map/all_to_all | solution.py:269
  114.8 4.3 %fold.1 = (f32[16,2,128]{2,1,0:T(2,128)}, f32[16,8,32]{2,1,0:T(8,128)}) custom-call(f32[32,32,128]{2,1,0:T(8,128)} %all_to_all.11.jr_ref, f32[8,16,256]{2,1,0:T(8,128)} %all_to_all.10.rr_ref), custom_call_target="tpu_custom_call" | custom-call | tf_op jit(solution)/shard_map/fold/pallas_call | solution.py:237
  (4 shorter events, 0.0 us)
Async XLA Ops:
  0.6 9.2 %copy-start = (bf16[16,16]{1,0:T(8,128)(2,1)S(1)}, bf16[16,16]{1,0:T(8,128)(2,1)}, u32[]{:S(2)}) copy-start(bf16[16,16]{1,0:T(8,128)(2,1)} %param.5) | copy-start | bytes 1540
  0.6 9.5 %copy-start.1 = (bf16[16,8]{0,1:T(8,128)(2,1)S(1)}, bf16[16,8]{0,1:T(8,128)(2,1)}, u32[]{:S(2)}) copy-start(bf16[16,8]{0,1:T(8,128)(2,1)} %param.4) | copy-start | bytes 772
  4.6 9.2 %collective-permute-start = (f32[64,3,128]{0,1,2:T(4,128)}, f32[64,3,128]{0,1,2:T(4,128)S(1)}, u32[]{:S(2)}, u32[]{:S(2)}) collective-permute-start(f32[64,3,128]{0,1,2:T(4,128)} %get-tuple-element.14), channel_id=1, source_target_pairs={{0,8},{8,16},{16,24},{24,32},{32,40},{40,48},{48,56},{56,64},{64,7... | collective-permute-start | bytes 294920 | tf_op jit(solution)/shard_map/ppermute | solution.py:22
  8.5 9.0 %collective-permute-start.1 = (f32[64,3,128]{0,1,2:T(4,128)}, f32[64,3,128]{0,1,2:T(4,128)S(1)}, u32[]{:S(2)}, u32[]{:S(2)}) collective-permute-start(f32[64,3,128]{0,1,2:T(4,128)} %get-tuple-element.15), channel_id=1, source_target_pairs={{8,0},{16,8},{24,16},{32,24},{40,32},{48,40},{56,48},{64,56},{72,6... | collective-permute-start | bytes 294920 | tf_op jit(solution)/shard_map/ppermute | solution.py:23
  18.2 7.9 %collective-permute-start.2 = (f32[64,38,3]{0,1,2:T(8,128)}, f32[64,38,3]{0,1,2:T(8,128)}, u32[]{:S(2)}, u32[]{:S(2)}) collective-permute-start(f32[64,38,3]{0,1,2:T(8,128)} %get-tuple-element.12), channel_id=1, source_target_pairs={{0,1},{1,2},{2,3},{3,4},{4,5},{5,6},{6,7},{8,9},{9,10},{10,11},{11... | collective-permute-start | bytes 87560 | tf_op jit(solution)/shard_map/ppermute | solution.py:22
  23.1 5.6 %collective-permute-start.3 = (f32[64,38,3]{0,1,2:T(8,128)S(1)}, f32[64,38,3]{0,1,2:T(8,128)}, u32[]{:S(2)}, u32[]{:S(2)}) collective-permute-start(f32[64,38,3]{0,1,2:T(8,128)S(1)} %get-tuple-element.13), channel_id=1, source_target_pairs={{1,0},{2,1},{3,2},{4,3},{5,4},{6,5},{7,6},{9,8},{10,9},{11,10},{12... | collective-permute-start | bytes 87560 | tf_op jit(solution)/shard_map/ppermute | solution.py:23

commit v2 on v1

v2 whole, which is shorter than its diff:
```python
import functools

import jax
import jax.numpy as jnp
from jax import lax
from jax.experimental import pallas as pl
from jax.experimental.pallas import tpu as pltpu
from jax.sharding import PartitionSpec as P

BANDS = 8
HID = 16
FEAT = 8
LOG2E = 1.4426950408889634
MESH = pl.DeviceIdType.MESH
GROUP = 4


def extended(shard, sides, width):
    for axis, dim in sides:
        peers, length = (lax.axis_size(axis), shard.shape[dim])
        up = [(i, i + 1) for i in range(peers - 1)]
        down = [(j, i) for i, j in up]
        last = lax.slice_in_dim(shard, length - width, length, axis=dim)
        initial = lax.slice_in_dim(shard, 0, width, axis=dim)
        before = lax.ppermute(last, axis, up)
        after = lax.ppermute(initial, axis, down)
        shard = jnp.concatenate([before, shard, after], axis=dim)
    return shard


def lanes_of():
    return lax.broadcasted_iota(jnp.int32, (8, 128), 1)


def softplus(v):
    grown = jnp.exp2(jnp.minimum(v * LOG2E, 126.0))
    return jnp.maximum(v, jnp.log(1.0 + grown))


def render(place_ref, tb_ref, w1_ref, w2_ref, j_ref, r_ref, s1_ref, p_ref, b_ref, d_ref, x_ref, u_ref, ch_ref, yc_ref, yt_ref, rs_ref):
    lane = lanes_of()
    seg = lax.broadcasted_iota(jnp.int32, (8, 128), 0)
    z = lane & 63
    half = lane >> 6
    top = z == 0
    bottom = z == 63
    full_x = place_ref[2]
    full_y = place_ref[3]
    at_x = place_ref[0] * 32 + half * 16
    at_y = place_ref[1] * 128 + seg * 16

    def above(v):
        return jnp.where(top, 0.0, pltpu.roll(v, 1, 1))

    def below(v):
        return jnp.where(bottom, 0.0, pltpu.roll(v, 127, 1))

    def inside(xp, yp):
        gy = at_y + yp
        ok = (gy >= 0) & (gy < full_y)
        if xp < 0:
            ok = ok & (at_x + xp >= 0)
        if xp > 15:
            ok = ok & (at_x + xp < full_x)
        return ok

    def field(xp, yp):
        return tb_ref[xp + 3, pl.ds(yp + 8, 8, stride=16), :]

    def first(yp):
        mid = [field(xp, yp) for xp in range(-3, 19)]
        for k in range(20):
            c = mid[k + 1]
            near = field(k - 2, yp - 1) + field(k - 2, yp + 1)
            near = near + (mid[k] + mid[k + 2]) + (above(c) + below(c))
            s1_ref[k, yp + 2] = jnp.where(inside(k - 2, yp), 0.4 * c + 0.1 * near, 0.0)

    def second(yp):
        mid = [s1_ref[k, yp + 2] for k in range(20)]
        for k in range(18):
            c = mid[k + 1]
            near = s1_ref[k + 1, yp + 1] + s1_ref[k + 1, yp + 3]
            near = near + (mid[k] + mid[k + 2]) + (above(c) + below(c))
            s = jnp.where(inside(k - 1, yp), 0.4 * c + 0.1 * near, 0.0)
            up, down = above(s), below(s)
            p_ref[k, yp + 1] = s
            b_ref[k, yp + 1] = 2.0 * s + (up + down)
            d_ref[k, yp + 1] = down - up

    one = jnp.ones((8, 128), jnp.float32)
    zero = jnp.zeros((8, 128), jnp.float32)

    def features(i, k):
        s = p_ref[i, k]
        a = p_ref[i + 1, k + 1] - p_ref[i - 1, k - 1]
        c = p_ref[i + 1, k - 1] - p_ref[i - 1, k + 1]
        gx = (b_ref[i + 1, k] - b_ref[i - 1, k] + (a + c)) * (1.0 / 3.0)
        gy = (b_ref[i, k + 1] - b_ref[i, k - 1] + (a - c)) * (1.0 / 3.0)
        d = d_ref[i, k]
        gz = (d + d + (d_ref[i + 1, k] + d_ref[i - 1, k]) + (d_ref[i, k + 1] + d_ref[i, k - 1])) * (1.0 / 3.0)
        q = 1.0 + gx * gx + gy * gy + gz * gz
        m = q * lax.rsqrt(q)
        return s, gx, gy, gz, m, s * m, s * s, one

    def first_layer(g, k):
        slot = g % 2
        for n in range(GROUP):
            rows = features(g * GROUP + n + 1, k + 1)
            for f in range(0, FEAT, 2):
                pair = jnp.concatenate([rows[f], rows[f + 1]], axis=0)
                x_ref[slot, 8 * f : 8 * f + 16, 128 * n : 128 * n + 128] = pair.astype(jnp.bfloat16)
        u_ref[slot] = jnp.dot(w1_ref[...], x_ref[slot], preferred_element_type=jnp.float32)

    def second_layer(g):
        slot = g % 2
        u = u_ref[slot]
        hidden = (u + u * jnp.tanh(u)).astype(jnp.bfloat16)
        ch_ref[slot] = jnp.dot(w2_ref[...], hidden, preferred_element_type=jnp.float32)

    def views(g, state):
        slot = g % 2
        for n in range(GROUP):
            row = (g * GROUP + n) * 8
            for b in range(BANDS):
                e = softplus(ch_ref[slot, 8 * b : 8 * b + 8, 128 * n : 128 * n + 128])
                t = softplus(ch_ref[slot, 64 + 8 * b : 72 + 8 * b, 128 * n : 128 * n + 128])
                q = jnp.exp2(t * (-LOG2E / 512.0))
                tx = state[8 + b]
                nx = tx * q
                state[b] = state[b] + (tx - nx) * e
                state[8 + b] = nx
                ty = yt_ref[b, row : row + 8, :]
                ny = ty * q
                yc_ref[b, row : row + 8, :] = yc_ref[b, row : row + 8, :] + (ty - ny) * e
                yt_ref[b, row : row + 8, :] = ny

    chunks = 16 // GROUP

    def columns(k, carry):
        state = [zero] * BANDS + [one] * BANDS
        for g in range(chunks):
            ahead = g + 2
            views(g, state)
            second_layer((g + 1) % chunks)
            first_layer(ahead % chunks, k + ahead // chunks)
        second(k + 3)
        first(k + 5)
        colour = [state[b] + state[8 + b] * pltpu.roll(state[b], 64, 1) for b in range(BANDS)]
        clear = [state[8 + b] * pltpu.roll(state[8 + b], 64, 1) for b in range(BANDS)]
        image = jnp.transpose(jnp.concatenate(colour + clear, axis=0))
        j_ref[pl.ds(k, 64, stride=16), :] = image[0:64]
        return carry

    def lead_first(i, carry):
        first(i - 2)
        return carry

    def lead_second(i, carry):
        second(i - 1)
        return carry

    lax.fori_loop(0, 7, lead_first, 0)
    lax.fori_loop(0, 4, lead_second, 0)
    for b in range(BANDS):
        yc_ref[b] = jnp.zeros((128, 128), jnp.float32)
        yt_ref[b] = jnp.ones((128, 128), jnp.float32)
    first_layer(0, 0)
    first_layer(1, 0)
    second_layer(0)
    lax.fori_loop(0, 16, columns, 0)

    for b in range(BANDS):
        for h in range(2):
            colour = yc_ref[b, pl.ds(64 * h, 8, stride=8), :]
            clear = yt_ref[b, pl.ds(64 * h, 8, stride=8), :]
            for s in range(1, 8):
                colour = colour + clear * yc_ref[b, pl.ds(64 * h + s, 8, stride=8), :]
                clear = clear * yt_ref[b, pl.ds(64 * h + s, 8, stride=8), :]
            rs_ref[0, 16 * b + 8 * h : 16 * b + 8 * h + 8, :] = colour
            rs_ref[1, 16 * b + 8 * h : 16 * b + 8 * h + 8, :] = clear
    for kind in range(2):
        image = jnp.transpose(rs_ref[kind])
        for h in range(2):
            for p in range(8):
                r_ref[p, h, :, 128 * kind : 128 * kind + 128] = image[64 * h + 8 * p : 64 * h + 8 * p + 8]


def render_call(place, tb, w1, w2):
    vmem = pl.BlockSpec(memory_space=pltpu.VMEM)
    return pl.pallas_call(
        render,
        out_shape=(
            jax.ShapeDtypeStruct((1024, 128), jnp.float32),
            jax.ShapeDtypeStruct((8, 2, 8, 256), jnp.float32),
        ),
        in_specs=[pl.BlockSpec(memory_space=pltpu.SMEM), vmem, vmem, vmem],
        out_specs=(vmem, vmem),
        scratch_shapes=[
            pltpu.VMEM((20, 23, 8, 128), jnp.float32),
            pltpu.VMEM((18, 20, 8, 128), jnp.float32),
            pltpu.VMEM((18, 20, 8, 128), jnp.float32),
            pltpu.VMEM((18, 20, 8, 128), jnp.float32),
            pltpu.VMEM((2, 64, 128 * GROUP), jnp.bfloat16),
            pltpu.VMEM((2, 128, 128 * GROUP), jnp.float32),
            pltpu.VMEM((2, 128, 128 * GROUP), jnp.float32),
            pltpu.VMEM((8, 128, 128), jnp.float32),
            pltpu.VMEM((8, 128, 128), jnp.float32),
            pltpu.VMEM((2, 128, 128), jnp.float32),
        ],
        compiler_params=pltpu.CompilerParams(vmem_limit_bytes=40 << 20),
        name="render",
    )(place, tb, w1, w2)


def fold(count_x, count_y, j_ref, r_ref, vx_ref, vy_ref, jr_ref, rr_ref, at_ref, send_x, recv_x, send_y, recv_y):
    me_x = lax.axis_index("bx")
    me_y = lax.axis_index("by")

    def peer_x(hop):
        return lax.rem(me_x + hop, count_x)

    def peer_y(hop):
        return lax.rem(me_y + hop, count_y)

    barrier = pltpu.get_barrier_semaphore()

    def greet_x(hop, carry):
        pl.semaphore_signal(barrier, inc=1, device_id=(peer_x(hop), me_y), device_id_type=MESH)
        return carry

    def greet_y(hop, carry):
        pl.semaphore_signal(barrier, inc=1, device_id=(me_x, peer_y(hop)), device_id_type=MESH)
        return carry

    lax.fori_loop(1, count_x, greet_x, 0)
    lax.fori_loop(1, count_y, greet_y, 0)
    pl.semaphore_wait(barrier, count_x + count_y - 2)

    def copy_x(peer, source, hop):
        return pltpu.make_async_remote_copy(
            src_ref=j_ref.at[peer],
            dst_ref=jr_ref.at[source],
            send_sem=send_x.at[hop],
            recv_sem=recv_x.at[source],
            device_id=(peer, me_y),
            device_id_type=MESH,
        )

    def copy_y(peer, source, hop):
        return pltpu.make_async_remote_copy(
            src_ref=r_ref.at[peer],
            dst_ref=rr_ref.at[source],
            send_sem=send_y.at[hop],
            recv_sem=recv_y.at[source],
            device_id=(me_x, peer),
            device_id_type=MESH,
        )

    def send_all_y(hop, carry):
        copy_y(peer_y(hop), me_y, hop).start()
        return carry

    def send_all_x(hop, carry):
        copy_x(peer_x(hop), me_x, hop).start()
        return carry

    lax.fori_loop(1, count_x, send_all_x, 0)
    lax.fori_loop(1, count_y, send_all_y, 0)
    jr_ref[me_x] = j_ref[me_x]
    rr_ref[me_y] = r_ref[me_y]

    lane = lax.broadcasted_iota(jnp.int32, (32, 128), 1)
    low = lane < 64

    def wait_y(hop, carry):
        copy_y(me_y, peer_y(hop), hop).wait_recv()
        return carry

    lax.fori_loop(1, count_y, wait_y, 0)

    def over_y(s, pair):
        piece = rr_ref[s]
        return pair[0] + pair[1] * piece[:, 0:128], pair[1] * piece[:, 128:256]

    start = (jnp.zeros((16, 128), jnp.float32), jnp.ones((16, 128), jnp.float32))
    kinds = lax.fori_loop(0, count_y, over_y, start)
    lane8 = lanes_of()
    for kind in range(2):
        for b in range(BANDS):
            shift = (128 - 16 * b) % 128
            front = kinds[kind][0:8]
            back = kinds[kind][8:16]
            front = pltpu.roll(front, shift, 1) if shift else front
            back = pltpu.roll(back, shift + 16, 1) if shift < 112 else back
            vy_ref[8 * kind + b] = jnp.where(lane8 < 16, front, back)[:, 0:32]

    def wait_x(hop, carry):
        copy_x(me_x, peer_x(hop), hop).wait_recv()
        return carry

    lax.fori_loop(1, count_x, wait_x, 0)

    def over(s, pair):
        front, clear = pair
        piece = jr_ref[s]
        both = jnp.where(low, pltpu.roll(piece, 64, 1), piece)
        return jnp.where(low, front, 0.0) + clear * piece, clear * both

    start = (jnp.zeros((32, 128), jnp.float32), jnp.ones((32, 128), jnp.float32))
    image, _ = lax.fori_loop(0, count_x, over, start)
    at_ref[0:32, :] = image
    at_ref[32:128, :] = jnp.zeros((96, 128), jnp.float32)
    at_ref[...] = jnp.transpose(at_ref[...])
    line = lax.broadcasted_iota(jnp.int32, (16, 128), 1)
    for z in range(2):
        row = jnp.zeros((16, 128), jnp.float32)
        for s in range(8):
            part = at_ref[pl.ds(s, 16, stride=8), :]
            shift = (16 * s - 16 * z) % 128
            part = pltpu.roll(part, shift, 1) if shift else part
            row = jnp.where((line >> 4) == s, part, row)
        vx_ref[:, z, :] = row

    def sent_x(hop, carry):
        copy_x(peer_x(hop), me_x, hop).wait_send()
        return carry

    def sent_y(hop, carry):
        copy_y(peer_y(hop), me_y, hop).wait_send()
        return carry

    lax.fori_loop(1, count_x, sent_x, 0)
    lax.fori_loop(1, count_y, sent_y, 0)


def fold_call(j, r):
    count_x = j.shape[0]
    count_y = r.shape[0]
    vmem = pl.BlockSpec(memory_space=pltpu.VMEM)
    return pl.pallas_call(
        functools.partial(fold, count_x, count_y),
        out_shape=(
            jax.ShapeDtypeStruct((16, 2, 128), jnp.float32),
            jax.ShapeDtypeStruct((16, 8, 32), jnp.float32),
        ),
        in_specs=[vmem, vmem],
        out_specs=(vmem, vmem),
        scratch_shapes=[
            pltpu.VMEM(j.shape, jnp.float32),
            pltpu.VMEM(r.shape, jnp.float32),
            pltpu.VMEM((128, 128), jnp.float32),
            pltpu.SemaphoreType.DMA((count_x,)),
            pltpu.SemaphoreType.DMA((count_x,)),
            pltpu.SemaphoreType.DMA((count_y,)),
            pltpu.SemaphoreType.DMA((count_y,)),
        ],
        compiler_params=pltpu.CompilerParams(collective_id=1, has_side_effects=True),
        name="fold",
    )(j, r)


def spread(weights, scale):
    rows, cols = weights.shape
    eye = jnp.eye(8, dtype=jnp.float32)
    big = (weights.astype(jnp.float32) * scale)[:, None, :, None] * eye[None, :, None, :]
    return big.reshape(rows * 8, cols * 8).astype(jnp.bfloat16)


def body(scalar_field, transfer_in, transfer_out):
    count_x = lax.axis_size("bx")
    count_y = lax.axis_size("by")
    wide = extended(scalar_field, (("bx", 1), ("by", 2)), 3)
    wide = jnp.pad(wide, ((0, 0), (0, 0), (5, 5)))
    halves = jnp.stack([wide[:, 0:22], wide[:, 16:38]])
    tb = jnp.transpose(halves, (2, 3, 0, 1)).reshape(22, 144, 128)
    place = jnp.stack(
        [lax.axis_index("bx"), lax.axis_index("by"), jnp.int32(32 * count_x), jnp.int32(128 * count_y)]
    ).astype(jnp.int32)
    j, r = render_call(place, tb, spread(transfer_in, 0.5), spread(transfer_out, 1.0))
    slab = 64 // count_x
    vx, vy = fold_call(j.reshape(count_x, slab * 16, 128), r.reshape(count_y, 128 // count_y, 256))
    return (vx.reshape(2, 8, slab, 128), vy.reshape(2, 8, 8, 32))


def solution(mesh):
    return jax.shard_map(
        body,
        mesh=mesh,
        in_specs=(P(None, "bx", "by"), P(), P()),
        out_specs=(P(None, None, "bx", "by"), P(None, None, "by", "bx")),
        check_vma=False,
    )
```

time: 121 us -> 92.5 us (0.76); the launches traced: 119 us -> 92 us
  blocking collectives: 37.9 us -> 0 us
  Pallas kernels: 43.3 us -> 49.5 us
  local copies, waits for them, and re-layouts: 12.4 us -> 17 us
    all_to_all x2 -> x0, blocking collectives: 37.9 us -> none  [the longest x1 28.4 us: body(): lax.all_to_all(j.reshape(count_x, slab * 16, 128), 'bx', split_axis=0, co...]
    pallas_call x1, Pallas kernels: 4.29 us -> 28.9 us  [fold_call(): pl.pallas_call(functools.partial(fold, count_x, count_y), out_shape=(jax....]
    pallas_call x1, Pallas kernels: 39 us -> 20.6 us  [render_call(): pl.pallas_call(render, out_shape=(jax.ShapeDtypeStruct((1024, 128), jnp.f...]
    unnamed x5 -> x11, local copies, waits for them, and re-layouts: 3.04 us -> 7.29 us
where the time goes in v2:
time: 92.5 us; the launch traced here: 92 us
  Pallas kernels  49.5 us (54%)
  local copies, waits for them, and re-layouts  17 us (18%)
  starting transfers between devices  12.1 us (13%)
  waiting for transfers between devices  9.98 us (11%)
  other arithmetic  2.61 us (3%)
    pallas_call x1, Pallas kernels, fold_call(): pl.pallas_call(functools.partial(fold, count_x, count_y), out_shape=(jax....  28.9 us
    pallas_call x1, Pallas kernels, render_call(): pl.pallas_call(render, out_shape=(jax.ShapeDtypeStruct((1024, 128), jnp.f...  20.6 us
    ppermute x2, starting transfers between devices, extended(): before = lax.ppermute(last, axis, up)  8.89 us
    unnamed x11, local copies, waits for them, and re-layouts  7.29 us
    ppermute x2, waiting for transfers between devices, extended(): after = lax.ppermute(initial, axis, down)  6.42 us
    transpose x1, local copies, waits for them, and re-layouts, body(): tb = jnp.transpose(halves, (2, 3, 0, 1)).reshape(22, 144, 128)  4.18 us
    ppermute x2, waiting for transfers between devices, extended(): before = lax.ppermute(last, axis, up)  3.55 us
    reshape x1, local copies, waits for them, and re-layouts, body(): tb = jnp.transpose(halves, (2, 3, 0, 1)).reshape(22, 144, 128)  3.46 us
  transfers between devices with their start and end apart: 4, of which 3 were waited for; matrix products, arithmetic and copies ran while one was open for 1% of the time, Pallas kernels for 0%

profile of v2, /device:TPU:1, one launch (start us, length us, event | category | flops | bytes accessed | tf_op | source)
XLA Modules:
  0.0 92.0 jit_solution(11864129473487345863)
XLA Ops:
  0.6 0.0 copy-start.2
  0.6 0.0 copy-start.3
  0.6 3.0 %copy.26 = f32[64,32,128]{0,1,2:T(8,128)S(1)} copy(f32[64,32,128]{2,1,0:T(8,128)} %param.3) | data formatting | bytes 2097152 | tf_op args[0]
  3.7 0.9 fusion.2
  4.6 3.9 %collective-permute-start = (f32[64,3,128]{0,1,2:T(4,128)}, f32[64,3,128]{0,1,2:T(4,128)S(1)}, u32[]{:S(2)}, u32[]{:S(2)}) collective-permute-start(f32[64,3,128]{0,1,2:T(4,128)} %get-tuple-element.14), channel_id=1, source_target_pairs={{0,8},{8,16},{16,24},{24,32},{32,40},{40,48},{48,56},{56,64},{64,7... | collective-permute-start | bytes 294920 | tf_op jit(solution)/shard_map/ppermute | solution.py:25
  8.5 1.3 %collective-permute-start.1 = (f32[64,3,128]{0,1,2:T(4,128)}, f32[64,3,128]{0,1,2:T(4,128)S(1)}, u32[]{:S(2)}, u32[]{:S(2)}) collective-permute-start(f32[64,3,128]{0,1,2:T(4,128)} %get-tuple-element.15), channel_id=1, source_target_pairs={{8,0},{16,8},{24,16},{32,24},{40,32},{48,40},{56,48},{64,56},{72,6... | collective-permute-start | bytes 294920 | tf_op jit(solution)/shard_map/ppermute | solution.py:26
  9.9 0.0 copy-done.2
  9.9 0.1 copy.30
  9.9 0.1 multiply_convert_fusion
  10.1 0.0 copy-done.3
  10.1 0.1 multiply_convert_fusion.1
  10.2 3.6 %collective-permute-done = f32[64,3,128]{0,1,2:T(4,128)S(1)} collective-permute-done((f32[64,3,128]{0,1,2:T(4,128)}, f32[64,3,128]{0,1,2:T(4,128)S(1)}, u32[]{:S(2)}, u32[]{:S(2)}) %collective-permute-start) | collective-permute-done | bytes 98336 | tf_op jit(solution)/shard_map/ppermute | solution.py:25
  13.8 3.7 %collective-permute-done.1 = f32[64,3,128]{0,1,2:T(4,128)S(1)} collective-permute-done((f32[64,3,128]{0,1,2:T(4,128)}, f32[64,3,128]{0,1,2:T(4,128)S(1)}, u32[]{:S(2)}, u32[]{:S(2)}) %collective-permute-start.1) | collective-permute-done | bytes 98336 | tf_op jit(solution)/shard_map/ppermute | solution.py:26
  17.5 0.6 pad_maximum_fusion.2
  18.2 4.9 %collective-permute-start.2 = (f32[64,38,3]{0,1,2:T(8,128)}, f32[64,38,3]{0,1,2:T(8,128)}, u32[]{:S(2)}, u32[]{:S(2)}) collective-permute-start(f32[64,38,3]{0,1,2:T(8,128)} %get-tuple-element.12), channel_id=1, source_target_pairs={{0,1},{1,2},{2,3},{3,4},{4,5},{5,6},{6,7},{8,9},{9,10},{10,11},{11... | collective-permute-start | bytes 87560 | tf_op jit(solution)/shard_map/ppermute | solution.py:25
  23.1 1.9 %collective-permute-start.3 = (f32[64,38,3]{0,1,2:T(8,128)S(1)}, f32[64,38,3]{0,1,2:T(8,128)}, u32[]{:S(2)}, u32[]{:S(2)}) collective-permute-start(f32[64,38,3]{0,1,2:T(8,128)S(1)} %get-tuple-element.13), channel_id=1, source_target_pairs={{1,0},{2,1},{3,2},{4,3},{5,4},{6,5},{7,6},{9,8},{10,9},{11,10},{12... | collective-permute-start | bytes 87560 | tf_op jit(solution)/shard_map/ppermute | solution.py:26
  25.0 0.1 pad_add_fusion.place_ref
  25.1 0.5 convert_element_type.34.w2_ref
  25.7 0.2 convert_element_type.31
  25.9 0.1 copy.31.w1_ref
  26.0 0.0 collective-permute-done.2
  26.0 2.7 %collective-permute-done.3 = f32[64,38,3]{0,1,2:T(8,128)} collective-permute-done((f32[64,38,3]{0,1,2:T(8,128)S(1)}, f32[64,38,3]{0,1,2:T(8,128)}, u32[]{:S(2)}, u32[]{:S(2)}) %collective-permute-start.3) | collective-permute-done | bytes 29216 | tf_op jit(solution)/shard_map/ppermute | solution.py:26
  28.8 1.4 %select_maximum_fusion = f32[64,38,144]{0,1,2:T(8,128)S(1)} fusion(f32[64,38,3]{0,1,2:T(8,128)} %collective-permute-done.3, f32[64,38,3]{0,1,2:T(8,128)} %collective-permute-done.2, f32[64,3,128]{0,1,2:T(4,128)S(1)} %collective-permute-done.1, f32[64,32,128]{0,1,2:T(8,128)S(1)} %copy.26, f32[64,3,128]{0,1,2:T(4,128)S(1)} %collective-permute-done), kind=kLoop, calls=%fused_computation.3 | loop fusion | flops 4202496 | bytes 2704384 | tf_op jit(solution)/shard_map/concatenate | solution.py:27
  30.1 0.2 slice_bitcast_fusion.1
  30.3 0.3 maximum_bitcast_fusion
  30.6 4.2 %copy.29 = f32[22,144,2,64]{3,2,1,0:T(2,128)} copy(f32[22,144,2,64]{3,0,1,2:T(8,128)S(1)} %maximum_bitcast_fusion) | data formatting | bytes 3244032 | tf_op jit(solution)/shard_map/transpose | solution.py:375
  34.8 3.5 %reshape.39.tb_ref = f32[22,144,128]{2,1,0:T(8,128)S(1)} reshape(f32[22,144,2,64]{3,2,1,0:T(2,128)} %copy.29) | data formatting | bytes 3244032 | tf_op jit(solution)/shard_map/reshape | solution.py:375
  38.3 20.6 %render.1 = (f32[1024,128]{1,0:T(8,128)S(1)}, f32[8,2,8,256]{3,2,1,0:T(8,128)S(1)}) custom-call(s32[4]{0:T(128)S(1)} %pad_add_fusion.place_ref, f32[22,144,128]{2,1,0:T(8,128)S(1)} %reshape.39.tb_ref, bf16[128,64]{1,0:T(8,128)(2,1)S(1)} %copy.31.w1_ref, bf16[128,128]{1,0:T(8,128)(2,1)S(1)} %convert_element_type.34.w2_ref), custom_call_target="tpu_custom_call" | custom-call | tf_op jit(solution)/shard_map/render/pallas_call | solution.py:190
  58.8 0.0 copy-start
  58.8 0.8 copy-done
  59.6 0.0 copy-start.1
  59.6 0.6 copy-done.1
  60.3 28.9 %fold.1 = (f32[16,2,128]{2,1,0:T(2,128)}, f32[16,8,32]{2,1,0:T(8,128)}) custom-call(f32[32,32,128]{2,1,0:T(8,128)} %bitcast.18, f32[8,16,256]{2,1,0:T(8,128)} %bitcast.19), custom_call_target="tpu_custom_call" | custom-call | tf_op jit(solution)/shard_map/fold/pallas_call | solution.py:340
  89.2 1.3 %copy.34 = f32[2,8,2,128]{3,2,1,0:T(2,128)} copy(f32[2,8,2,128]{3,2,1,0:T(2,128)} %bitcast.21) | data formatting | bytes 32768
  90.5 1.5 %copy.35 = f32[2,8,8,32]{3,2,1,0:T(8,128)} copy(f32[2,8,8,32]{3,2,1,0:T(8,128)} %bitcast.20) | data formatting | bytes 32768
  (4 shorter events, 0.0 us)
Async XLA Ops:
  0.6 9.2 %copy-start.2 = (bf16[16,16]{1,0:T(8,128)(2,1)S(1)}, bf16[16,16]{1,0:T(8,128)(2,1)}, u32[]{:S(2)}) copy-start(bf16[16,16]{1,0:T(8,128)(2,1)} %param.5) | copy-start | bytes 1540
  0.6 9.5 %copy-start.3 = (bf16[16,8]{0,1:T(8,128)(2,1)S(1)}, bf16[16,8]{0,1:T(8,128)(2,1)}, u32[]{:S(2)}) copy-start(bf16[16,8]{0,1:T(8,128)(2,1)} %param.4) | copy-start | bytes 772
  4.6 9.2 %collective-permute-start = (f32[64,3,128]{0,1,2:T(4,128)}, f32[64,3,128]{0,1,2:T(4,128)S(1)}, u32[]{:S(2)}, u32[]{:S(2)}) collective-permute-start(f32[64,3,128]{0,1,2:T(4,128)} %get-tuple-element.14), channel_id=1, source_target_pairs={{0,8},{8,16},{16,24},{24,32},{32,40},{40,48},{48,56},{56,64},{64,7... | collective-permute-start | bytes 294920 | tf_op jit(solution)/shard_map/ppermute | solution.py:25
  8.5 9.0 %collective-permute-start.1 = (f32[64,3,128]{0,1,2:T(4,128)}, f32[64,3,128]{0,1,2:T(4,128)S(1)}, u32[]{:S(2)}, u32[]{:S(2)}) collective-permute-start(f32[64,3,128]{0,1,2:T(4,128)} %get-tuple-element.15), channel_id=1, source_target_pairs={{8,0},{16,8},{24,16},{32,24},{40,32},{48,40},{56,48},{64,56},{72,6... | collective-permute-start | bytes 294920 | tf_op jit(solution)/shard_map/ppermute | solution.py:26
  18.2 7.9 %collective-permute-start.2 = (f32[64,38,3]{0,1,2:T(8,128)}, f32[64,38,3]{0,1,2:T(8,128)}, u32[]{:S(2)}, u32[]{:S(2)}) collective-permute-start(f32[64,38,3]{0,1,2:T(8,128)} %get-tuple-element.12), channel_id=1, source_target_pairs={{0,1},{1,2},{2,3},{3,4},{4,5},{5,6},{6,7},{8,9},{9,10},{10,11},{11... | collective-permute-start | bytes 87560 | tf_op jit(solution)/shard_map/ppermute | solution.py:25
  23.1 5.6 %collective-permute-start.3 = (f32[64,38,3]{0,1,2:T(8,128)S(1)}, f32[64,38,3]{0,1,2:T(8,128)}, u32[]{:S(2)}, u32[]{:S(2)}) collective-permute-start(f32[64,38,3]{0,1,2:T(8,128)S(1)} %get-tuple-element.13), channel_id=1, source_target_pairs={{1,0},{2,1},{3,2},{4,3},{5,4},{6,5},{7,6},{9,8},{10,9},{11,10},{12... | collective-permute-start | bytes 87560 | tf_op jit(solution)/shard_map/ppermute | solution.py:26
  58.8 0.8 copy-start
  59.6 0.7 copy-start.1

commit v3 on v2

--- a/solution.py
+++ b/solution.py
@@ -15,19 +15,6 @@
 GROUP = 4
 
 
-def extended(shard, sides, width):
-    for axis, dim in sides:
-        peers, length = (lax.axis_size(axis), shard.shape[dim])
-        up = [(i, i + 1) for i in range(peers - 1)]
-        down = [(j, i) for i, j in up]
-        last = lax.slice_in_dim(shard, length - width, length, axis=dim)
-        initial = lax.slice_in_dim(shard, 0, width, axis=dim)
-        before = lax.ppermute(last, axis, up)
-        after = lax.ppermute(initial, axis, down)
-        shard = jnp.concatenate([before, shard, after], axis=dim)
-    return shard
-
-
 def lanes_of():
     return lax.broadcasted_iota(jnp.int32, (8, 128), 1)
 
@@ -35,6 +22,126 @@
 def softplus(v):
     grown = jnp.exp2(jnp.minimum(v * LOG2E, 126.0))
     return jnp.maximum(v, jnp.log(1.0 + grown))
+
+
+def halo(count_x, count_y, f_ref, tb_ref, xs_ref, xr_ref, yr_ref, cr_ref, sx, rx, sy, ry, sc, rc):
+    me_x = lax.axis_index("bx")
+    me_y = lax.axis_index("by")
+    xs = (lax.rem(me_x + count_x - 1, count_x), lax.rem(me_x + 1, count_x))
+    ys = (lax.rem(me_y + count_y - 1, count_y), lax.rem(me_y + 1, count_y))
+
+    barrier = pltpu.get_barrier_semaphore()
+    for peer in [(x, me_y) for x in xs] + [(me_x, y) for y in ys] + [(x, y) for x in xs for y in ys]:
+        pl.semaphore_signal(barrier, inc=1, device_id=peer, device_id_type=MESH)
+
+    def plane(x):
+        return f_ref[pl.ds(x, 64, stride=32), :]
+
+    for i in range(3):
+        xs_ref[0, i] = plane(i)
+        xs_ref[1, i] = plane(29 + i)
+    pl.semaphore_wait(barrier, 8)
+
+    copies = []
+    for side in range(2):
+        copies.append(
+            pltpu.make_async_remote_copy(
+                src_ref=xs_ref.at[side],
+                dst_ref=xr_ref.at[1 - side],
+                send_sem=sx.at[side],
+                recv_sem=rx.at[1 - side],
+                device_id=(xs[side], me_y),
+                device_id_type=MESH,
+            )
+        )
+        copies[-1].start()
+
+    def turn(x, front, back):
+        tb_ref[x + 3, 8:136, :] = jnp.transpose(jnp.concatenate([front, back], axis=0))
+
+    edges = (pl.ds(8, 8), pl.ds(128, 8))
+    ends = (pl.ds(3, 3), pl.ds(16, 3))
+    for x in (0, 1, 2, 13, 14, 15):
+        turn(x, plane(x), plane(16 + x))
+    for side in range(2):
+        for part in range(2):
+            copies.append(
+                pltpu.make_async_remote_copy(
+                    src_ref=tb_ref.at[ends[side], edges[part]],
+                    dst_ref=cr_ref.at[2 * (1 - side) + (1 - part)],
+                    send_sem=sc.at[2 * side + part],
+                    recv_sem=rc.at[2 * (1 - side) + (1 - part)],
+                    device_id=(xs[side], ys[part]),
+                    device_id_type=MESH,
+                )
+            )
+            copies[-1].start()
+
+    def rest(x, carry):
+        turn(x, plane(x), plane(16 + x))
+        return carry
+
+    lax.fori_loop(3, 13, rest, 0)
+    for part in range(2):
+        copies.append(
+            pltpu.make_async_remote_copy(
+                src_ref=tb_ref.at[pl.ds(3, 16), edges[part]],
+                dst_ref=yr_ref.at[1 - part],
+                send_sem=sy.at[part],
+                recv_sem=ry.at[1 - part],
+                device_id=(me_x, ys[part]),
+                device_id_type=MESH,
+            )
+        )
+        copies[-1].start()
+
+    inner_x = (me_x > 0, me_x < count_x - 1)
+    inner_y = (me_y > 0, me_y < count_y - 1)
+    copies[0].wait_recv()
+    copies[1].wait_recv()
+    for i in range(3):
+        turn(i - 3, jnp.where(inner_x[0], xr_ref[0, i], 0.0), plane(13 + i))
+        turn(16 + i, plane(16 + i), jnp.where(inner_x[1], xr_ref[1, i], 0.0))
+    for copy in copies[2:]:
+        copy.wait_recv()
+    low = lax.broadcasted_iota(jnp.int32, (8, 128), 1) < 64
+    rims = (pl.ds(0, 8), pl.ds(136, 8))
+    for part in range(2):
+        for x in range(16):
+            tb_ref[x + 3, rims[part], :] = jnp.where(inner_y[part], yr_ref[part, x], 0.0)
+        for i in range(3):
+            far = jnp.where(inner_x[0], cr_ref[part, i], 0.0)
+            edge = jnp.where(low, pltpu.roll(far, 64, 1), pltpu.roll(yr_ref[part, 13 + i], 64, 1))
+            tb_ref[i, rims[part], :] = jnp.where(inner_y[part], edge, 0.0)
+            far = jnp.where(inner_x[1], cr_ref[2 + part, i], 0.0)
+            edge = jnp.where(low, pltpu.roll(yr_ref[part, i], 64, 1), pltpu.roll(far, 64, 1))
+            tb_ref[19 + i, rims[part], :] = jnp.where(inner_y[part], edge, 0.0)
+    for copy in copies:
+        copy.wait_send()
+
+
+def halo_call(field, count_x, count_y):
+    vmem = pl.BlockSpec(memory_space=pltpu.VMEM)
+    return pl.pallas_call(
+        functools.partial(halo, count_x, count_y),
+        out_shape=jax.ShapeDtypeStruct((22, 144, 128), jnp.float32),
+        in_specs=[vmem],
+        out_specs=vmem,
+        scratch_shapes=[
+            pltpu.VMEM((2, 3, 64, 128), jnp.float32),
+            pltpu.VMEM((2, 3, 64, 128), jnp.float32),
+            pltpu.VMEM((2, 16, 8, 128), jnp.float32),
+            pltpu.VMEM((4, 3, 8, 128), jnp.float32),
+            pltpu.SemaphoreType.DMA((2,)),
+            pltpu.SemaphoreType.DMA((2,)),
+            pltpu.SemaphoreType.DMA((2,)),
+            pltpu.SemaphoreType.DMA((2,)),
+            pltpu.SemaphoreType.DMA((4,)),
+            pltpu.SemaphoreType.DMA((4,)),
+        ],
+        compiler_params=pltpu.CompilerParams(collective_id=0, has_side_effects=True),
+        name="halo",
+    )(field)
 
 
 def render(place_ref, tb_ref, w1_ref, w2_ref, j_ref, r_ref, s1_ref, p_ref, b_ref, d_ref, x_ref, u_ref, ch_ref, yc_ref, yt_ref, rs_ref):
@@ -207,12 +314,12 @@
             pltpu.VMEM((8, 128, 128), jnp.float32),
             pltpu.VMEM((2, 128, 128), jnp.float32),
         ],
-        compiler_params=pltpu.CompilerParams(vmem_limit_bytes=40 << 20),
+        compiler_params=pltpu.CompilerParams(vmem_limit_bytes=20 << 20),
         name="render",
     )(place, tb, w1, w2)
 
 
-def fold(count_x, count_y, j_ref, r_ref, vx_ref, vy_ref, jr_ref, rr_ref, at_ref, send_x, recv_x, send_y, recv_y):
+def exchange(count_x, count_y, j_ref, r_ref, jr_ref, rr_ref, send_x, recv_x, send_y, recv_y):
     me_x = lax.axis_index("bx")
     me_y = lax.axis_index("by")
 
@@ -269,14 +376,54 @@
     jr_ref[me_x] = j_ref[me_x]
     rr_ref[me_y] = r_ref[me_y]
 
+    def wait_y(hop, carry):
+        copy_y(me_y, peer_y(hop), hop).wait_recv()
+        return carry
+
+    def wait_x(hop, carry):
+        copy_x(me_x, peer_x(hop), hop).wait_recv()
+        return carry
+
+    def sent_x(hop, carry):
+        copy_x(peer_x(hop), me_x, hop).wait_send()
+        return carry
+
+    def sent_y(hop, carry):
+        copy_y(peer_y(hop), me_y, hop).wait_send()
+        return carry
+
+    lax.fori_loop(1, count_x, sent_x, 0)
+    lax.fori_loop(1, count_y, sent_y, 0)
+    lax.fori_loop(1, count_y, wait_y, 0)
+    lax.fori_loop(1, count_x, wait_x, 0)
+
+
+def exchange_call(j, r):
+    count_x = j.shape[0]
+    count_y = r.shape[0]
+    vmem = pl.BlockSpec(memory_space=pltpu.VMEM)
+    return pl.pallas_call(
+        functools.partial(exchange, count_x, count_y),
+        out_shape=(
+            jax.ShapeDtypeStruct(j.shape, jnp.float32),
+            jax.ShapeDtypeStruct(r.shape, jnp.float32),
+        ),
+        in_specs=[vmem, vmem],
+        out_specs=(vmem, vmem),
+        scratch_shapes=[
+            pltpu.SemaphoreType.DMA((count_x,)),
+            pltpu.SemaphoreType.DMA((count_x,)),
+            pltpu.SemaphoreType.DMA((count_y,)),
+            pltpu.SemaphoreType.DMA((count_y,)),
+        ],
+        compiler_params=pltpu.CompilerParams(collective_id=1, has_side_effects=True),
+        name="exchange",
+    )(j, r)
+
+
+def fold(count_x, count_y, jr_ref, rr_ref, vx_ref, vy_ref, at_ref):
     lane = lax.broadcasted_iota(jnp.int32, (32, 128), 1)
     low = lane < 64
-
-    def wait_y(hop, carry):
-        copy_y(me_y, peer_y(hop), hop).wait_recv()
-        return carry
-
-    lax.fori_loop(1, count_y, wait_y, 0)
 
     def over_y(s, pair):
         piece = rr_ref[s]
@@ -293,12 +440,6 @@
             front = pltpu.roll(front, shift, 1) if shift else front
             back = pltpu.roll(back, shift + 16, 1) if shift < 112 else back
             vy_ref[8 * kind + b] = jnp.where(lane8 < 16, front, back)[:, 0:32]
-
-    def wait_x(hop, carry):
-        copy_x(me_x, peer_x(hop), hop).wait_recv()
-        return carry
-
-    lax.fori_loop(1, count_x, wait_x, 0)
 
     def over(s, pair):
         front, clear = pair
@@ -321,42 +462,20 @@
             row = jnp.where((line >> 4) == s, part, row)
         vx_ref[:, z, :] = row
 
-    def sent_x(hop, carry):
-        copy_x(peer_x(hop), me_x, hop).wait_send()
-        return carry
-
-    def sent_y(hop, carry):
-        copy_y(peer_y(hop), me_y, hop).wait_send()
-        return carry
-
-    lax.fori_loop(1, count_x, sent_x, 0)
-    lax.fori_loop(1, count_y, sent_y, 0)
-
-
-def fold_call(j, r):
-    count_x = j.shape[0]
-    count_y = r.shape[0]
+
+def fold_call(jr, rr):
     vmem = pl.BlockSpec(memory_space=pltpu.VMEM)
     return pl.pallas_call(
-        functools.partial(fold, count_x, count_y),
+        functools.partial(fold, jr.shape[0], rr.shape[0]),
         out_shape=(
             jax.ShapeDtypeStruct((16, 2, 128), jnp.float32),
             jax.ShapeDtypeStruct((16, 8, 32), jnp.float32),
         ),
         in_specs=[vmem, vmem],
         out_specs=(vmem, vmem),
-        scratch_shapes=[
-            pltpu.VMEM(j.shape, jnp.float32),
-            pltpu.VMEM(r.shape, jnp.float32),
-            pltpu.VMEM((128, 128), jnp.float32),
-            pltpu.SemaphoreType.DMA((count_x,)),
-            pltpu.SemaphoreType.DMA((count_x,)),
-            pltpu.SemaphoreType.DMA((count_y,)),
-            pltpu.SemaphoreType.DMA((count_y,)),
-        ],
-        compiler_params=pltpu.CompilerParams(collective_id=1, has_side_effects=True),
+        scratch_shapes=[pltpu.VMEM((128, 128), jnp.float32)],
         name="fold",
-    )(j, r)
+    )(jr, rr)
 
 
 def spread(weights, scale):
@@ -369,16 +488,14 @@
 def body(scalar_field, transfer_in, transfer_out):
     count_x = lax.axis_size("bx")
     count_y = lax.axis_size("by")
-    wide = extended(scalar_field, (("bx", 1), ("by", 2)), 3)
-    wide = jnp.pad(wide, ((0, 0), (0, 0), (5, 5)))
-    halves = jnp.stack([wide[:, 0:22], wide[:, 16:38]])
-    tb = jnp.transpose(halves, (2, 3, 0, 1)).reshape(22, 144, 128)
+    tb = halo_call(scalar_field.reshape(2048, 128), count_x, count_y)
     place = jnp.stack(
         [lax.axis_index("bx"), lax.axis_index("by"), jnp.int32(32 * count_x), jnp.int32(128 * count_y)]
     ).astype(jnp.int32)
     j, r = render_call(place, tb, spread(transfer_in, 0.5), spread(transfer_out, 1.0))
     slab = 64 // count_x
-    vx, vy = fold_call(j.reshape(count_x, slab * 16, 128), r.reshape(count_y, 128 // count_y, 256))
+    jr, rr = exchange_call(j.reshape(count_x, slab * 16, 128), r.reshape(count_y, 128 // count_y, 256))
+    vx, vy = fold_call(jr, rr)
     return (vx.reshape(2, 8, slab, 128), vy.reshape(2, 8, 8, 32))
 
 

time: 92.5 us -> 68.7 us (0.74)
  the two profiles are of different devices: /device:TPU:1 before, /device:TPU:6 now
where the time goes in v3:
time: 68.7 us; the launch traced here: 68.4 us
  Pallas kernels  62.2 us (91%)
  local copies, waits for them, and re-layouts  3.8 us (6%)
  other arithmetic  1.73 us (3%)
  between operations  0.71 us (1%)
    pallas_call x1, Pallas kernels, exchange_call(): pl.pallas_call(functools.partial(exchange, count_x, count_y), out_shape=(...  25 us
    pallas_call x1, Pallas kernels, render_call(): pl.pallas_call(render, out_shape=(jax.ShapeDtypeStruct((1024, 128), jnp.f...  20.4 us
    pallas_call x1, Pallas kernels, halo_call(): pl.pallas_call(functools.partial(halo, count_x, count_y), out_shape=jax.S...  12.5 us
    pallas_call x1, Pallas kernels, fold_call(): pl.pallas_call(functools.partial(fold, jr.shape[0], rr.shape[0]), out_sha...  4.26 us
    unnamed x6, local copies, waits for them, and re-layouts  2.84 us

profile of v3, /device:TPU:6, one launch (start us, length us, event | category | flops | bytes accessed | tf_op | source)
XLA Modules:
  0.0 68.4 jit_solution(15098975513765254223)
XLA Ops:
  0.6 0.1 pad_add_fusion.place_ref
  0.7 0.1 copy.6
  0.8 0.7 %convert_multiply_fusion = f32[16,8]{0,1:T(8,128)S(1)} fusion(bf16[16,8]{0,1:T(8,128)(2,1)} %param.4), kind=kLoop, calls=%fused_computation.3 | loop fusion | flops 256 | bytes 768 | tf_op jit(solution)/shard_map/mul | solution.py:484
  1.5 0.7 %convert_element_type.30 = f32[16,16]{1,0:T(8,128)S(1)} convert(bf16[16,16]{1,0:T(8,128)(2,1)} %param.5) | non-fusion elementwise | flops 256 | bytes 1536 | tf_op jit(solution)/shard_map/convert_element_type | solution.py:484
  2.2 0.1 multiply_convert_fusion.1
  2.3 0.2 convert_element_type.29
  2.5 0.1 copy.7.w1_ref
  2.7 0.2 multiply_convert_fusion
  2.8 0.5 convert_element_type.32.w2_ref
  3.4 12.5 %halo.1.tb_ref = f32[22,144,128]{2,1,0:T(8,128)} custom-call(f32[2048,128]{1,0:T(8,128)} %bitcast.15), custom_call_target="tpu_custom_call" | custom-call | tf_op jit(solution)/shard_map/halo/pallas_call | solution.py:125
  15.9 0.0 copy-start
  15.9 1.4 %copy-done = f32[22,144,128]{2,1,0:T(8,128)S(1)} copy-done((f32[22,144,128]{2,1,0:T(8,128)S(1)}, f32[22,144,128]{2,1,0:T(8,128)}, u32[]{:S(2)}) %copy-start) | copy-done | bytes 1622040
  17.3 20.4 %render.1 = (f32[1024,128]{1,0:T(8,128)S(1)}, f32[8,2,8,256]{3,2,1,0:T(8,128)S(1)}) custom-call(s32[4]{0:T(128)S(1)} %pad_add_fusion.place_ref, f32[22,144,128]{2,1,0:T(8,128)S(1)} %copy-done, bf16[128,64]{1,0:T(8,128)(2,1)S(1)} %copy.7.w1_ref, bf16[128,128]{1,0:T(8,128)(2,1)S(1)} %convert_element_type.32.w2_ref), custom_call_target="tpu_custom_call" | custom-call | tf_op jit(solution)/shard_map/render/pallas_call | solution.py:297
  37.7 0.0 copy-start.1
  37.8 0.8 %copy-done.1 = f32[1024,128]{1,0:T(8,128)} copy-done((f32[1024,128]{1,0:T(8,128)}, f32[1024,128]{1,0:T(8,128)S(1)}, u32[]{:S(2)}) %copy-start.1) | copy-done | bytes 524312
  38.5 0.0 copy-start.2
  38.5 0.6 copy-done.2
  39.2 25.0 %exchange.1 = (f32[32,32,128]{2,1,0:T(8,128)}, f32[8,16,256]{2,1,0:T(8,128)}) custom-call(f32[32,32,128]{2,1,0:T(8,128)} %bitcast.13, f32[8,16,256]{2,1,0:T(8,128)} %bitcast.14), custom_call_target="tpu_custom_call" | custom-call | tf_op jit(solution)/shard_map/exchange/pallas_call | solution.py:405
  64.2 4.3 %fold.1 = (f32[16,2,128]{2,1,0:T(2,128)}, f32[16,8,32]{2,1,0:T(8,128)}) custom-call(f32[32,32,128]{2,1,0:T(8,128)} %get-tuple-element.10.jr_ref, f32[8,16,256]{2,1,0:T(8,128)} %get-tuple-element.11.rr_ref), custom_call_target="tpu_custom_call" | custom-call | tf_op jit(solution)/shard_map/fold/pallas_call | solution.py:468
  (2 shorter events, 0.0 us)
Async XLA Ops:
  15.9 1.4 %copy-start = (f32[22,144,128]{2,1,0:T(8,128)S(1)}, f32[22,144,128]{2,1,0:T(8,128)}, u32[]{:S(2)}) copy-start(f32[22,144,128]{2,1,0:T(8,128)} %halo.1.tb_ref) | copy-start | bytes 4866052
  37.7 0.8 %copy-start.1 = (f32[1024,128]{1,0:T(8,128)}, f32[1024,128]{1,0:T(8,128)S(1)}, u32[]{:S(2)}) copy-start(f32[1024,128]{1,0:T(8,128)S(1)} %get-tuple-element.8) | copy-start | bytes 1572868
  38.5 0.6 copy-start.2

commit v4 on v3

v4 whole, which is shorter than its diff:
```python
import functools

import jax
import jax.numpy as jnp
from jax import lax
from jax.experimental import pallas as pl
from jax.experimental.pallas import tpu as pltpu
from jax.sharding import PartitionSpec as P

BANDS = 8
HID = 16
FEAT = 8
LOG2E = 1.4426950408889634
MESH = pl.DeviceIdType.MESH
GROUP = 4


def lanes_of():
    return lax.broadcasted_iota(jnp.int32, (8, 128), 1)


def softplus(v):
    grown = jnp.exp2(jnp.minimum(v * LOG2E, 126.0))
    return jnp.maximum(v, jnp.log(1.0 + grown))


def widen(big_ref, weights_ref, scale):
    rows, cols = weights_ref.shape
    up = lax.broadcasted_iota(jnp.int32, (8 * rows, rows), 0) >> 3
    up = (up == lax.broadcasted_iota(jnp.int32, (8 * rows, rows), 1)).astype(jnp.float32)
    out = lax.broadcasted_iota(jnp.int32, (cols, 8 * cols), 1) >> 3
    out = (out == lax.broadcasted_iota(jnp.int32, (cols, 8 * cols), 0)).astype(jnp.float32)
    tall = jnp.dot(up.astype(jnp.bfloat16), weights_ref[...], preferred_element_type=jnp.float32)
    wide = jnp.dot(tall.astype(jnp.bfloat16), out.astype(jnp.bfloat16), preferred_element_type=jnp.float32)
    at_row = lax.broadcasted_iota(jnp.int32, wide.shape, 0) & 7
    at_col = lax.broadcasted_iota(jnp.int32, wide.shape, 1) & 7
    big_ref[...] = jnp.where(at_row == at_col, wide * scale, 0.0).astype(jnp.bfloat16)


def march(
    count_x, count_y, f_ref, win_ref, wout_ref, vx_ref, vy_ref,
    tb_ref, xs_ref, xr_ref, yr_ref, cr_ref,
    w1_ref, w2_ref, s1_ref, p_ref, b_ref, d_ref, x_ref, u_ref, ch_ref, yc_ref, yt_ref, rs_ref,
    j_ref, jr_ref, r_ref, rr_ref, at_ref,
    sx, rx, sy, ry, sc, rc, send_x, recv_x, send_y, recv_y,
):
    me_x = lax.axis_index("bx")
    me_y = lax.axis_index("by")
    xs = (lax.rem(me_x + count_x - 1, count_x), lax.rem(me_x + 1, count_x))
    ys = (lax.rem(me_y + count_y - 1, count_y), lax.rem(me_y + 1, count_y))

    def peer_x(hop):
        return lax.rem(me_x + hop, count_x)

    def peer_y(hop):
        return lax.rem(me_y + hop, count_y)

    barrier = pltpu.get_barrier_semaphore()

    def greet_x(hop, carry):
        pl.semaphore_signal(barrier, inc=1, device_id=(peer_x(hop), me_y), device_id_type=MESH)
        return carry

    def greet_y(hop, carry):
        pl.semaphore_signal(barrier, inc=1, device_id=(me_x, peer_y(hop)), device_id_type=MESH)
        return carry

    for x in xs:
        for y in ys:
            pl.semaphore_signal(barrier, inc=1, device_id=(x, y), device_id_type=MESH)
    lax.fori_loop(1, count_x, greet_x, 0)
    lax.fori_loop(1, count_y, greet_y, 0)

    def plane(x):
        return f_ref[pl.ds(x, 64, stride=32), :]

    for i in range(3):
        xs_ref[0, i] = plane(i)
        xs_ref[1, i] = plane(29 + i)
    widen(w1_ref, win_ref, 0.5)
    widen(w2_ref, wout_ref, 1.0)
    pl.semaphore_wait(barrier, count_x + count_y + 2)

    copies = []
    for side in range(2):
        copies.append(
            pltpu.make_async_remote_copy(
                src_ref=xs_ref.at[side],
                dst_ref=xr_ref.at[1 - side],
                send_sem=sx.at[side],
                recv_sem=rx.at[1 - side],
                device_id=(xs[side], me_y),
                device_id_type=MESH,
            )
        )
        copies[-1].start()

    def turn(x, front, back):
        tb_ref[x + 3, 8:136, :] = jnp.transpose(jnp.concatenate([front, back], axis=0))

    edges = (pl.ds(8, 8), pl.ds(128, 8))
    ends = (pl.ds(3, 3), pl.ds(16, 3))
    for x in (0, 1, 2, 13, 14, 15):
        turn(x, plane(x), plane(16 + x))
    for side in range(2):
        for part in range(2):
            copies.append(
                pltpu.make_async_remote_copy(
                    src_ref=tb_ref.at[ends[side], edges[part]],
                    dst_ref=cr_ref.at[2 * (1 - side) + (1 - part)],
                    send_sem=sc.at[2 * side + part],
                    recv_sem=rc.at[2 * (1 - side) + (1 - part)],
                    device_id=(xs[side], ys[part]),
                    device_id_type=MESH,
                )
            )
            copies[-1].start()

    def rest(x, carry):
        turn(x, plane(x), plane(16 + x))
        return carry

    lax.fori_loop(3, 13, rest, 0)
    for part in range(2):
        copies.append(
            pltpu.make_async_remote_copy(
                src_ref=tb_ref.at[pl.ds(3, 16), edges[part]],
                dst_ref=yr_ref.at[1 - part],
                send_sem=sy.at[part],
                recv_sem=ry.at[1 - part],
                device_id=(me_x, ys[part]),
                device_id_type=MESH,
            )
        )
        copies[-1].start()

    inner_x = (me_x > 0, me_x < count_x - 1)
    inner_y = (me_y > 0, me_y < count_y - 1)
    copies[0].wait_recv()
    copies[1].wait_recv()
    for i in range(3):
        turn(i - 3, jnp.where(inner_x[0], xr_ref[0, i], 0.0), plane(13 + i))
        turn(16 + i, plane(16 + i), jnp.where(inner_x[1], xr_ref[1, i], 0.0))
    for copy in copies[2:]:
        copy.wait_recv()
    low = lanes_of() < 64
    rims = (pl.ds(0, 8), pl.ds(136, 8))
    for part in range(2):
        for x in range(16):
            tb_ref[x + 3, rims[part], :] = jnp.where(inner_y[part], yr_ref[part, x], 0.0)
        for i in range(3):
            far = jnp.where(inner_x[0], cr_ref[part, i], 0.0)
            edge = jnp.where(low, pltpu.roll(far, 64, 1), pltpu.roll(yr_ref[part, 13 + i], 64, 1))
            tb_ref[i, rims[part], :] = jnp.where(inner_y[part], edge, 0.0)
            far = jnp.where(inner_x[1], cr_ref[2 + part, i], 0.0)
            edge = jnp.where(low, pltpu.roll(yr_ref[part, i], 64, 1), pltpu.roll(far, 64, 1))
            tb_ref[19 + i, rims[part], :] = jnp.where(inner_y[part], edge, 0.0)
    for copy in copies:
        copy.wait_send()

    lane = lanes_of()
    seg = lax.broadcasted_iota(jnp.int32, (8, 128), 0)
    z = lane & 63
    half = lane >> 6
    top = z == 0
    bottom = z == 63
    full_x = 32 * count_x
    full_y = 128 * count_y
    at_x = me_x * 32 + half * 16
    at_y = me_y * 128 + seg * 16

    def above(v):
        return jnp.where(top, 0.0, pltpu.roll(v, 1, 1))

    def below(v):
        return jnp.where(bottom, 0.0, pltpu.roll(v, 127, 1))

    def inside(xp, yp):
        gy = at_y + yp
        ok = (gy >= 0) & (gy < full_y)
        if xp < 0:
            ok = ok & (at_x + xp >= 0)
        if xp > 15:
            ok = ok & (at_x + xp < full_x)
        return ok

    def field(xp, yp):
        return tb_ref[xp + 3, pl.ds(yp + 8, 8, stride=16), :]

    def first(yp):
        mid = [field(xp, yp) for xp in range(-3, 19)]
        for k in range(20):
            c = mid[k + 1]
            near = field(k - 2, yp - 1) + field(k - 2, yp + 1)
            near = near + (mid[k] + mid[k + 2]) + (above(c) + below(c))
            s1_ref[k, yp + 2] = jnp.where(inside(k - 2, yp), 0.4 * c + 0.1 * near, 0.0)

    def second(yp):
        mid = [s1_ref[k, yp + 2] for k in range(20)]
        for k in range(18):
            c = mid[k + 1]
            near = s1_ref[k + 1, yp + 1] + s1_ref[k + 1, yp + 3]
            near = near + (mid[k] + mid[k + 2]) + (above(c) + below(c))
            s = jnp.where(inside(k - 1, yp), 0.4 * c + 0.1 * near, 0.0)
            up, down = above(s), below(s)
            p_ref[k, yp + 1] = s
            b_ref[k, yp + 1] = 2.0 * s + (up + down)
            d_ref[k, yp + 1] = down - up

    one = jnp.ones((8, 128), jnp.float32)
    zero = jnp.zeros((8, 128), jnp.float32)

    def features(i, k):
        s = p_ref[i, k]
        a = p_ref[i + 1, k + 1] - p_ref[i - 1, k - 1]
        c = p_ref[i + 1, k - 1] - p_ref[i - 1, k + 1]
        gx = (b_ref[i + 1, k] - b_ref[i - 1, k] + (a + c)) * (1.0 / 3.0)
        gy = (b_ref[i, k + 1] - b_ref[i, k - 1] + (a - c)) * (1.0 / 3.0)
        d = d_ref[i, k]
        gz = (d + d + (d_ref[i + 1, k] + d_ref[i - 1, k]) + (d_ref[i, k + 1] + d_ref[i, k - 1])) * (1.0 / 3.0)
        q = 1.0 + gx * gx + gy * gy + gz * gz
        m = q * lax.rsqrt(q)
        return s, gx, gy, gz, m, s * m, s * s, one

    def first_layer(g, k):
        slot = g
        for n in range(GROUP):
            rows = features(g * GROUP + n + 1, k + 1)
            for f in range(0, FEAT, 2):
                pair = jnp.concatenate([rows[f], rows[f + 1]], axis=0)
                x_ref[slot, 8 * f : 8 * f + 16, 128 * n : 128 * n + 128] = pair.astype(jnp.bfloat16)
        u_ref[slot] = jnp.dot(w1_ref[...], x_ref[slot], preferred_element_type=jnp.float32)

    def second_layer(g):
        slot = g
        u = u_ref[slot]
        hidden = (u + u * jnp.tanh(u)).astype(jnp.bfloat16)
        ch_ref[slot] = jnp.dot(w2_ref[...], hidden, preferred_element_type=jnp.float32)

    def views(g, state):
        slot = g
        for n in range(GROUP):
            row = (g * GROUP + n) * 8
            for b in range(BANDS):
                e = softplus(ch_ref[slot, 8 * b : 8 * b + 8, 128 * n : 128 * n + 128])
                t = softplus(ch_ref[slot, 64 + 8 * b : 72 + 8 * b, 128 * n : 128 * n + 128])
                q = jnp.exp2(t * (-LOG2E / 512.0))
                tx = state[8 + b]
                nx = tx * q
                state[b] = state[b] + (tx - nx) * e
                state[8 + b] = nx
                ty = yt_ref[b, row : row + 8, :]
                ny = ty * q
                yc_ref[b, row : row + 8, :] = yc_ref[b, row : row + 8, :] + (ty - ny) * e
                yt_ref[b, row : row + 8, :] = ny

    chunks = 16 // GROUP

    def column(k):
        state = [zero] * BANDS + [one] * BANDS
        for g in range(chunks):
            views(g, state)
            second_layer((g + 2) % chunks)
            first_layer((g + 4) % chunks, k + (g + 4) // chunks)
        second(k + 3)
        first(k + 5)
        colour = [state[b] + state[8 + b] * pltpu.roll(state[b], 64, 1) for b in range(BANDS)]
        clear = [state[8 + b] * pltpu.roll(state[8 + b], 64, 1) for b in range(BANDS)]
        image = jnp.transpose(jnp.concatenate(colour + clear, axis=0))
        j_ref[pl.ds((k // 4) * 256 + k % 4, 64, stride=4), :] = image[0:64]

    def lead_first(i, carry):
        first(i - 2)
        return carry

    def lead_second(i, carry):
        second(i - 1)
        return carry

    def slab(start):
        return pl.ds(pl.multiple_of(start, 8), 8)

    def send_slabs(c):
        def one_peer(hop, carry):
            peer = peer_x(hop)
            pltpu.make_async_remote_copy(
                src_ref=j_ref.at[slab(c * 256 + peer * 8)],
                dst_ref=jr_ref.at[slab(c * 256 + me_x * 8)],
                send_sem=send_x.at[c],
                recv_sem=recv_x.at[c],
                device_id=(peer, me_y),
                device_id_type=MESH,
            ).start()
            return carry

        lax.fori_loop(1, count_x, one_peer, 0)
        jr_ref[slab(c * 256 + me_x * 8), :] = j_ref[slab(c * 256 + me_x * 8), :]

    def slabs_moved(c):
        many = pl.ds(0, (count_x - 1) * 8)
        return pltpu.make_async_remote_copy(
            src_ref=j_ref.at[many],
            dst_ref=jr_ref.at[many],
            send_sem=send_x.at[c],
            recv_sem=recv_x.at[c],
            device_id=(xs[1], me_y),
            device_id_type=MESH,
        )

    def rows_moved():
        many = pl.ds(0, count_y - 1)
        return pltpu.make_async_remote_copy(
            src_ref=r_ref.at[many],
            dst_ref=rr_ref.at[many],
            send_sem=send_y,
            recv_sem=recv_y,
            device_id=(me_x, ys[1]),
            device_id_type=MESH,
        )

    lax.fori_loop(0, 7, lead_first, 0)
    lax.fori_loop(0, 4, lead_second, 0)
    for b in range(BANDS):
        yc_ref[b] = jnp.zeros((128, 128), jnp.float32)
        yt_ref[b] = jnp.ones((128, 128), jnp.float32)
    for g in range(4):
        first_layer(g, 0)
    for g in range(2):
        second_layer(g)

    def part(c, carry):
        def one_column(n, carry):
            column(4 * c + n)
            return carry

        lax.fori_loop(0, 4, one_column, 0)
        send_slabs(c)
        return carry

    lax.fori_loop(0, 4, part, 0)

    for b in range(BANDS):
        for h in range(2):
            colour = yc_ref[b, pl.ds(64 * h, 8, stride=8), :]
            clear = yt_ref[b, pl.ds(64 * h, 8, stride=8), :]
            for s in range(1, 8):
                colour = colour + clear * yc_ref[b, pl.ds(64 * h + s, 8, stride=8), :]
                clear = clear * yt_ref[b, pl.ds(64 * h + s, 8, stride=8), :]
            rs_ref[0, 16 * b + 8 * h : 16 * b + 8 * h + 8, :] = colour
            rs_ref[1, 16 * b + 8 * h : 16 * b + 8 * h + 8, :] = clear
    for kind in range(2):
        image = jnp.transpose(rs_ref[kind])
        for h in range(2):
            for p in range(8):
                r_ref[p, 8 * h : 8 * h + 8, 128 * kind : 128 * kind + 128] = image[64 * h + 8 * p : 64 * h + 8 * p + 8]


    def send_rows(hop, carry):
        peer = peer_y(hop)
        pltpu.make_async_remote_copy(
            src_ref=r_ref.at[peer],
            dst_ref=rr_ref.at[me_y],
            send_sem=send_y,
            recv_sem=recv_y,
            device_id=(me_x, peer),
            device_id_type=MESH,
        ).start()
        return carry

    lax.fori_loop(1, count_y, send_rows, 0)
    rr_ref[me_y] = r_ref[me_y]

    at_ref[...] = jnp.zeros_like(at_ref)

    def fold_x(c):
        slabs_moved(c).wait_recv()
        image, clear = zero, one
        for s in range(count_x):
            piece = jr_ref[c * 256 + s * 8 : c * 256 + s * 8 + 8, :]
            both = jnp.where(low, pltpu.roll(piece, 64, 1), piece)
            image = jnp.where(low, image, 0.0) + clear * piece
            clear = clear * both
        for z in range(2):
            at_ref[16 * z + 4 * c : 16 * z + 4 * c + 4, :] = image[4 * z : 4 * z + 4]

    for c in range(3):
        fold_x(c)

    rows_moved().wait_recv()
    colour, clear = rr_ref[0, :, 0:128], rr_ref[0, :, 128:256]
    for s in range(1, count_y):
        colour = colour + clear * rr_ref[s, :, 0:128]
        clear = clear * rr_ref[s, :, 128:256]
    for kind, image in enumerate((colour, clear)):
        for b in range(BANDS):
            shift = (128 - 16 * b) % 128
            front = image[0:8]
            back = image[8:16]
            front = pltpu.roll(front, shift, 1) if shift else front
            back = pltpu.roll(back, shift + 16, 1) if shift < 112 else back
            vy_ref[8 * kind + b] = jnp.where(lane < 16, front, back)[:, 0:32]

    fold_x(3)
    at_ref[...] = jnp.transpose(at_ref[...])
    line = lax.broadcasted_iota(jnp.int32, (16, 128), 1)
    for z in range(2):
        row = jnp.zeros((16, 128), jnp.float32)
        for s in range(8):
            piece = at_ref[pl.ds(s, 16, stride=8), :]
            shift = (16 * s - 16 * z) % 128
            piece = pltpu.roll(piece, shift, 1) if shift else piece
            row = jnp.where((line >> 4) == s, piece, row)
        vx_ref[:, z, :] = row

    for c in range(4):
        slabs_moved(c).wait_send()
    rows_moved().wait_send()


def march_call(field, transfer_in, transfer_out, count_x, count_y):
    vmem = pl.BlockSpec(memory_space=pltpu.VMEM)

    def held(*shape, dtype=jnp.float32):
        return pltpu.VMEM(shape, dtype)

    return pl.pallas_call(
        functools.partial(march, count_x, count_y),
        out_shape=(
            jax.ShapeDtypeStruct((16, 2, 128), jnp.float32),
            jax.ShapeDtypeStruct((16, 8, 32), jnp.float32),
        ),
        in_specs=[vmem] * 3,
        out_specs=(vmem, vmem),
        scratch_shapes=[
            held(22, 144, 128),
            held(2, 3, 64, 128),
            held(2, 3, 64, 128),
            held(2, 16, 8, 128),
            held(4, 3, 8, 128),
            held(128, 64, dtype=jnp.bfloat16),
            held(128, 128, dtype=jnp.bfloat16),
            held(20, 23, 8, 128),
            held(18, 20, 8, 128),
            held(18, 20, 8, 128),
            held(18, 20, 8, 128),
            held(16 // GROUP, 64, 128 * GROUP, dtype=jnp.bfloat16),
            held(16 // GROUP, 128, 128 * GROUP),
            held(16 // GROUP, 128, 128 * GROUP),
            held(8, 128, 128),
            held(8, 128, 128),
            held(2, 128, 128),
            held(1024, 128),
            held(1024, 128),
            held(8, 16, 256),
            held(8, 16, 256),
            held(128, 128),
            pltpu.SemaphoreType.DMA((2,)),
            pltpu.SemaphoreType.DMA((2,)),
            pltpu.SemaphoreType.DMA((2,)),
            pltpu.SemaphoreType.DMA((2,)),
            pltpu.SemaphoreType.DMA((4,)),
            pltpu.SemaphoreType.DMA((4,)),
            pltpu.SemaphoreType.DMA((4,)),
            pltpu.SemaphoreType.DMA((4,)),
            pltpu.SemaphoreType.DMA,
            pltpu.SemaphoreType.DMA,
        ],
        compiler_params=pltpu.CompilerParams(collective_id=0, has_side_effects=True, vmem_limit_bytes=40 << 20),
        name="march",
    )(field, transfer_in, transfer_out)


def emit(ax_ref, ay_ref, vx_ref, vy_ref):
    vx_ref[...] = ax_ref[...]
    vy_ref[...] = ay_ref[...]


def emit_call(ax, ay):
    vmem = pl.BlockSpec(memory_space=pltpu.VMEM)
    return pl.pallas_call(
        emit,
        out_shape=(jax.ShapeDtypeStruct(ax.shape, ax.dtype), jax.ShapeDtypeStruct(ay.shape, ay.dtype)),
        in_specs=[vmem, vmem],
        out_specs=(vmem, vmem),
        name="emit",
    )(ax, ay)


def body(scalar_field, transfer_in, transfer_out):
    count_x = lax.axis_size("bx")
    count_y = lax.axis_size("by")
    ax, ay = march_call(scalar_field.reshape(2048, 128), transfer_in, transfer_out, count_x, count_y)
    vx, vy = emit_call(ax, ay)
    return (vx.reshape(2, 8, 2, 128), vy.reshape(2, 8, 8, 32))


def solution(mesh):
    return jax.shard_map(
        body,
        mesh=mesh,
        in_specs=(P(None, "bx", "by"), P(), P()),
        out_specs=(P(None, None, "bx", "by"), P(None, None, "by", "bx")),
        check_vma=False,
    )
```

time: 68.7 us -> 48.5 us (0.71)
  the two profiles are of different devices: /device:TPU:6 before, /device:TPU:1 now
where the time goes in v4:
time: 48.5 us; the launch traced here: 47.9 us
  Pallas kernels  44.1 us (91%)
  local copies, waits for them, and re-layouts  3.2 us (7%)
  between operations  0.66 us (1%)
    pallas_call x1, Pallas kernels, march_call(): pl.pallas_call(functools.partial(march, count_x, count_y), out_shape=(jax...  42.6 us
    unnamed x9, local copies, waits for them, and re-layouts  3.2 us
    pallas_call x1, Pallas kernels, emit_call(): pl.pallas_call(emit, out_shape=(jax.ShapeDtypeStruct(ax.shape, ax.dtype),...  1.49 us

profile of v4, /device:TPU:1, one launch (start us, length us, event | category | flops | bytes accessed | tf_op | source)
XLA Modules:
  0.0 47.9 jit_solution(18207183494632785046)
XLA Ops:
  0.6 0.0 copy-start.3
  0.6 0.8 %copy.5.win_ref = bf16[16,8]{1,0:T(8,128)(2,1)S(1)} copy(bf16[16,8]{0,1:T(8,128)(2,1)} %param.4) | data formatting | bytes 512 | tf_op args[1]
  1.4 0.0 copy-done.3
  1.4 0.0 copy-start
  1.4 1.2 %copy-done = f32[64,32,128]{2,1,0:T(8,128)S(1)} copy-done((f32[64,32,128]{2,1,0:T(8,128)S(1)}, f32[64,32,128]{2,1,0:T(8,128)}, u32[]{:S(2)}) %copy-start) | copy-done | bytes 1048600
  2.6 42.6 %march.1 = (f32[16,2,128]{2,1,0:T(2,128)S(1)}, f32[16,8,32]{2,1,0:T(8,128)S(1)}) custom-call(f32[2048,128]{1,0:T(8,128)S(1)} %bitcast.3, bf16[16,8]{1,0:T(8,128)(2,1)S(1)} %copy.5.win_ref, bf16[16,16]{1,0:T(8,128)(2,1)S(1)} %copy-done.3), custom_call_target="tpu_custom_call" | custom-call | tf_op jit(solution)/shard_map/march/pallas_call | solution.py:426
  45.2 0.0 copy-start.1
  45.2 0.6 %copy-done.1 = f32[16,8,32]{2,1,0:T(8,128)} copy-done((f32[16,8,32]{2,1,0:T(8,128)}, f32[16,8,32]{2,1,0:T(8,128)S(1)}, u32[]{:S(2)}) %copy-start.1) | copy-done | bytes 16408
  45.9 0.0 copy-start.2
  45.9 0.6 %copy-done.2 = f32[16,2,128]{2,1,0:T(2,128)} copy-done((f32[16,2,128]{2,1,0:T(2,128)}, f32[16,2,128]{2,1,0:T(2,128)S(1)}, u32[]{:S(2)}) %copy-start.2) | copy-done | bytes 16408
  46.5 1.5 %emit.1 = (f32[16,2,128]{2,1,0:T(2,128)}, f32[16,8,32]{2,1,0:T(8,128)}) custom-call(f32[16,2,128]{2,1,0:T(2,128)} %copy-done.2, f32[16,8,32]{2,1,0:T(8,128)} %copy-done.1), custom_call_target="tpu_custom_call" | custom-call | tf_op jit(solution)/shard_map/emit/pallas_call | solution.py:480
Async XLA Ops:
  0.6 0.8 %copy-start.3 = (bf16[16,16]{1,0:T(8,128)(2,1)S(1)}, bf16[16,16]{1,0:T(8,128)(2,1)}, u32[]{:S(2)}) copy-start(bf16[16,16]{1,0:T(8,128)(2,1)} %wout_ref.1) | copy-start | bytes 1540
  1.4 1.2 %copy-start = (f32[64,32,128]{2,1,0:T(8,128)S(1)}, f32[64,32,128]{2,1,0:T(8,128)}, u32[]{:S(2)}) copy-start(f32[64,32,128]{2,1,0:T(8,128)} %param.3) | copy-start | bytes 3145732
  45.2 0.6 %copy-start.1 = (f32[16,8,32]{2,1,0:T(8,128)}, f32[16,8,32]{2,1,0:T(8,128)S(1)}, u32[]{:S(2)}) copy-start(f32[16,8,32]{2,1,0:T(8,128)S(1)} %get-tuple-element.7.ay_ref) | copy-start | bytes 49156
  45.9 0.6 %copy-start.2 = (f32[16,2,128]{2,1,0:T(2,128)}, f32[16,2,128]{2,1,0:T(2,128)S(1)}, u32[]{:S(2)}) copy-start(f32[16,2,128]{2,1,0:T(2,128)S(1)} %get-tuple-element.6.ax_ref) | copy-start | bytes 49156

commit v5 on v4

--- a/solution.py
+++ b/solution.py
@@ -11,6 +11,7 @@
 HID = 16
 FEAT = 8
 LOG2E = 1.4426950408889634
+LN2 = 0.6931471805599453
 MESH = pl.DeviceIdType.MESH
 GROUP = 4
 
@@ -20,17 +21,19 @@
 
 
 def softplus(v):
-    grown = jnp.exp2(jnp.minimum(v * LOG2E, 126.0))
-    return jnp.maximum(v, jnp.log(1.0 + grown))
+    v = v * LOG2E
+    return jnp.maximum(v, lax.log2(1.0 + jnp.exp2(jnp.minimum(v, 126.0))))
 
 
 def widen(big_ref, weights_ref, scale):
-    rows, cols = weights_ref.shape
+    cols, rows = weights_ref.shape
     up = lax.broadcasted_iota(jnp.int32, (8 * rows, rows), 0) >> 3
     up = (up == lax.broadcasted_iota(jnp.int32, (8 * rows, rows), 1)).astype(jnp.float32)
     out = lax.broadcasted_iota(jnp.int32, (cols, 8 * cols), 1) >> 3
     out = (out == lax.broadcasted_iota(jnp.int32, (cols, 8 * cols), 0)).astype(jnp.float32)
-    tall = jnp.dot(up.astype(jnp.bfloat16), weights_ref[...], preferred_element_type=jnp.float32)
+    tall = lax.dot_general(
+        up.astype(jnp.bfloat16), weights_ref[...], (((1,), (1,)), ((), ())), preferred_element_type=jnp.float32
+    )
     wide = jnp.dot(tall.astype(jnp.bfloat16), out.astype(jnp.bfloat16), preferred_element_type=jnp.float32)
     at_row = lax.broadcasted_iota(jnp.int32, wide.shape, 0) & 7
     at_col = lax.broadcasted_iota(jnp.int32, wide.shape, 1) & 7
@@ -38,10 +41,10 @@
 
 
 def march(
-    count_x, count_y, f_ref, win_ref, wout_ref, vx_ref, vy_ref,
+    count_x, count_y, field_ref, win_ref, wout_ref, vx_ref, vy_ref,
     tb_ref, xs_ref, xr_ref, yr_ref, cr_ref,
     w1_ref, w2_ref, s1_ref, p_ref, b_ref, d_ref, x_ref, u_ref, ch_ref, yc_ref, yt_ref, rs_ref,
-    j_ref, jr_ref, r_ref, rr_ref, at_ref,
+    j_ref, jr_ref, r_ref, rr_ref, at_ref, st_ref, f_ref, load,
     sx, rx, sy, ry, sc, rc, send_x, recv_x, send_y, recv_y,
 ):
     me_x = lax.axis_index("bx")
@@ -55,6 +58,8 @@
     def peer_y(hop):
         return lax.rem(me_y + hop, count_y)
 
+    fetch = pltpu.make_async_copy(field_ref, f_ref, load)
+    fetch.start()
     barrier = pltpu.get_barrier_semaphore()
 
     def greet_x(hop, carry):
@@ -74,11 +79,12 @@
     def plane(x):
         return f_ref[pl.ds(x, 64, stride=32), :]
 
+    widen(w1_ref, win_ref, 0.5)
+    widen(w2_ref, wout_ref, 1.0)
+    fetch.wait()
     for i in range(3):
         xs_ref[0, i] = plane(i)
         xs_ref[1, i] = plane(29 + i)
-    widen(w1_ref, win_ref, 0.5)
-    widen(w2_ref, wout_ref, 1.0)
     pl.semaphore_wait(barrier, count_x + count_y + 2)
 
     copies = []
@@ -116,11 +122,8 @@
             )
             copies[-1].start()
 
-    def rest(x, carry):
+    for x in range(3, 13):
         turn(x, plane(x), plane(16 + x))
-        return carry
-
-    lax.fori_loop(3, 13, rest, 0)
     for part in range(2):
         copies.append(
             pltpu.make_async_remote_copy(
@@ -244,7 +247,7 @@
             for b in range(BANDS):
                 e = softplus(ch_ref[slot, 8 * b : 8 * b + 8, 128 * n : 128 * n + 128])
                 t = softplus(ch_ref[slot, 64 + 8 * b : 72 + 8 * b, 128 * n : 128 * n + 128])
-                q = jnp.exp2(t * (-LOG2E / 512.0))
+                q = jnp.exp2(t * (-1.0 / 512.0))
                 tx = state[8 + b]
                 nx = tx * q
                 state[b] = state[b] + (tx - nx) * e
@@ -256,7 +259,16 @@
 
     chunks = 16 // GROUP
 
+    def deliver(row):
+        state = [st_ref[b] for b in range(2 * BANDS)]
+        colour = [(state[b] + state[8 + b] * pltpu.roll(state[b], 64, 1)) * LN2 for b in range(BANDS)]
+        clear = [state[8 + b] * pltpu.roll(state[8 + b], 64, 1) for b in range(BANDS)]
+        image = jnp.transpose(jnp.concatenate(colour + clear, axis=0))
+        j_ref[pl.ds(row, 64, stride=4), :] = image[0:64]
+
     def column(k):
+        past = (k + 15) // 16
+        deliver(past * (((k + 3) // 4 - 1) * 256 + (k + 3) % 4) + (1 - past) * 1024)
         state = [zero] * BANDS + [one] * BANDS
         for g in range(chunks):
             views(g, state)
@@ -264,18 +276,8 @@
             first_layer((g + 4) % chunks, k + (g + 4) // chunks)
         second(k + 3)
         first(k + 5)
-        colour = [state[b] + state[8 + b] * pltpu.roll(state[b], 64, 1) for b in range(BANDS)]
-        clear = [state[8 + b] * pltpu.roll(state[8 + b], 64, 1) for b in range(BANDS)]
-        image = jnp.transpose(jnp.concatenate(colour + clear, axis=0))
-        j_ref[pl.ds((k // 4) * 256 + k % 4, 64, stride=4), :] = image[0:64]
-
-    def lead_first(i, carry):
-        first(i - 2)
-        return carry
-
-    def lead_second(i, carry):
-        second(i - 1)
-        return carry
+        for b in range(2 * BANDS):
+            st_ref[b] = state[b]
 
     def slab(start):
         return pl.ds(pl.multiple_of(start, 8), 8)
@@ -293,7 +295,8 @@
             ).start()
             return carry
 
-        lax.fori_loop(1, count_x, one_peer, 0)
+        for hop in range(1, count_x):
+            one_peer(hop, 0)
         jr_ref[slab(c * 256 + me_x * 8), :] = j_ref[slab(c * 256 + me_x * 8), :]
 
     def slabs_moved(c):
@@ -318,8 +321,10 @@
             device_id_type=MESH,
         )
 
-    lax.fori_loop(0, 7, lead_first, 0)
-    lax.fori_loop(0, 4, lead_second, 0)
+    for yp in range(-2, 5):
+        first(yp)
+    for yp in range(-1, 3):
+        second(yp)
     for b in range(BANDS):
         yc_ref[b] = jnp.zeros((128, 128), jnp.float32)
         yt_ref[b] = jnp.ones((128, 128), jnp.float32)
@@ -328,16 +333,18 @@
     for g in range(2):
         second_layer(g)
 
-    def part(c, carry):
-        def one_column(n, carry):
-            column(4 * c + n)
-            return carry
-
-        lax.fori_loop(0, 4, one_column, 0)
-        send_slabs(c)
+    def one_column(k, carry):
+        column(k)
+
+        @pl.when((k > 0) & (k % 4 == 0))
+        def _():
+            send_slabs(k // 4 - 1)
+
         return carry
 
-    lax.fori_loop(0, 4, part, 0)
+    lax.fori_loop(0, 16, one_column, 0)
+    deliver(3 * 256 + 3)
+    send_slabs(3)
 
     for b in range(BANDS):
         for h in range(2):
@@ -346,7 +353,7 @@
             for s in range(1, 8):
                 colour = colour + clear * yc_ref[b, pl.ds(64 * h + s, 8, stride=8), :]
                 clear = clear * yt_ref[b, pl.ds(64 * h + s, 8, stride=8), :]
-            rs_ref[0, 16 * b + 8 * h : 16 * b + 8 * h + 8, :] = colour
+            rs_ref[0, 16 * b + 8 * h : 16 * b + 8 * h + 8, :] = colour * LN2
             rs_ref[1, 16 * b + 8 * h : 16 * b + 8 * h + 8, :] = clear
     for kind in range(2):
         image = jnp.transpose(rs_ref[kind])
@@ -429,7 +436,7 @@
             jax.ShapeDtypeStruct((16, 2, 128), jnp.float32),
             jax.ShapeDtypeStruct((16, 8, 32), jnp.float32),
         ),
-        in_specs=[vmem] * 3,
+        in_specs=[pl.BlockSpec(memory_space=pltpu.HBM), vmem, vmem],
         out_specs=(vmem, vmem),
         scratch_shapes=[
             held(22, 144, 128),
@@ -449,11 +456,14 @@
             held(8, 128, 128),
             held(8, 128, 128),
             held(2, 128, 128),
-            held(1024, 128),
+            held(1280, 128),
             held(1024, 128),
             held(8, 16, 256),
             held(8, 16, 256),
             held(128, 128),
+            held(16, 8, 128),
+            held(2048, 128),
+            pltpu.SemaphoreType.DMA,
             pltpu.SemaphoreType.DMA((2,)),
             pltpu.SemaphoreType.DMA((2,)),
             pltpu.SemaphoreType.DMA((2,)),
@@ -465,23 +475,28 @@
             pltpu.SemaphoreType.DMA,
             pltpu.SemaphoreType.DMA,
         ],
-        compiler_params=pltpu.CompilerParams(collective_id=0, has_side_effects=True, vmem_limit_bytes=40 << 20),
+        compiler_params=pltpu.CompilerParams(collective_id=0, has_side_effects=True, vmem_limit_bytes=24 << 20),
         name="march",
     )(field, transfer_in, transfer_out)
 
 
-def emit(ax_ref, ay_ref, vx_ref, vy_ref):
-    vx_ref[...] = ax_ref[...]
-    vy_ref[...] = ay_ref[...]
+def emit(ax_ref, ay_ref, vx_ref, vy_ref, done):
+    moves = (pltpu.make_async_copy(ax_ref, vx_ref, done.at[0]), pltpu.make_async_copy(ay_ref, vy_ref, done.at[1]))
+    for move in moves:
+        move.start()
+    for move in moves:
+        move.wait()
 
 
 def emit_call(ax, ay):
-    vmem = pl.BlockSpec(memory_space=pltpu.VMEM)
+    anywhere = pl.BlockSpec(memory_space=pl.ANY)
     return pl.pallas_call(
         emit,
         out_shape=(jax.ShapeDtypeStruct(ax.shape, ax.dtype), jax.ShapeDtypeStruct(ay.shape, ay.dtype)),
-        in_specs=[vmem, vmem],
-        out_specs=(vmem, vmem),
+        in_specs=[anywhere, anywhere],
+        out_specs=(anywhere, anywhere),
+        scratch_shapes=[pltpu.SemaphoreType.DMA((2,))],
+        compiler_params=pltpu.CompilerParams(vmem_limit_bytes=1 << 20),
         name="emit",
     )(ax, ay)
 
@@ -489,7 +504,9 @@
 def body(scalar_field, transfer_in, transfer_out):
     count_x = lax.axis_size("bx")
     count_y = lax.axis_size("by")
-    ax, ay = march_call(scalar_field.reshape(2048, 128), transfer_in, transfer_out, count_x, count_y)
+    ax, ay = march_call(
+        scalar_field.reshape(2048, 128), transfer_in.T, transfer_out.T, count_x, count_y
+    )
     vx, vy = emit_call(ax, ay)
     return (vx.reshape(2, 8, 2, 128), vy.reshape(2, 8, 8, 32))
 

time: 48.5 us -> 43.4 us (0.89)
  Pallas kernels: 44.1 us -> 40.6 us
  local copies, waits for them, and re-layouts: 3.2 us -> 2 us
    pallas_call x1, Pallas kernels: 42.6 us -> 39.9 us  [march_call(): pl.pallas_call(functools.partial(march, count_x, count_y), out_shape=(jax...]
    unnamed x9 -> x5, local copies, waits for them, and re-layouts: 3.2 us -> 2 us
    pallas_call x1, Pallas kernels: 1.49 us -> 0.65 us  [emit_call(): pl.pallas_call(emit, out_shape=(jax.ShapeDtypeStruct(ax.shape, ax.dtype),...]
where the time goes in v5:
time: 43.4 us; the launch traced here: 43.2 us
  Pallas kernels  40.6 us (94%)
  local copies, waits for them, and re-layouts  2 us (5%)
  between operations  0.65 us (1%)
    pallas_call x1, Pallas kernels, march_call(): pl.pallas_call(functools.partial(march, count_x, count_y), out_shape=(jax...  39.9 us
    unnamed x5, local copies, waits for them, and re-layouts  2 us

profile of v5, /device:TPU:1, one launch (start us, length us, event | category | flops | bytes accessed | tf_op | source)
XLA Modules:
  0.0 43.2 jit_solution(2567148181041319733)
XLA Ops:
  0.6 0.0 copy-start.1
  0.6 0.8 %copy.5 = bf16[16,16]{0,1:T(8,128)(2,1)S(1)} copy(bf16[16,16]{1,0:T(8,128)(2,1)} %param.5) | data formatting | bytes 1024 | tf_op args[2]
  1.4 0.0 copy-done.1
  1.4 0.0 copy-start
  1.4 1.2 %copy-done = f32[64,32,128]{2,1,0:T(8,128)S(1)} copy-done((f32[64,32,128]{2,1,0:T(8,128)S(1)}, f32[64,32,128]{2,1,0:T(8,128)}, u32[]{:S(2)}) %copy-start) | copy-done | bytes 1048600
  2.6 39.9 %march.1 = (f32[16,2,128]{2,1,0:T(2,128)S(1)}, f32[16,8,32]{2,1,0:T(8,128)S(1)}) custom-call(f32[2048,128]{1,0:T(8,128)S(1)} %bitcast.5, bf16[8,16]{1,0:T(8,128)(2,1)S(1)} %bitcast.7, bf16[16,16]{1,0:T(8,128)(2,1)S(1)} %bitcast.6), custom_call_target="tpu_custom_call" | custom-call | tf_op jit(solution)/shard_map/march/pallas_call | solution.py:433
  42.6 0.7 %emit.1 = (f32[16,2,128]{2,1,0:T(2,128)}, f32[16,8,32]{2,1,0:T(8,128)}) custom-call(f32[16,2,128]{2,1,0:T(2,128)S(1)} %get-tuple-element.6.ax_ref, f32[16,8,32]{2,1,0:T(8,128)S(1)} %get-tuple-element.7.ay_ref), custom_call_target="tpu_custom_call" | custom-call | tf_op jit(solution)/shard_map/emit/pallas_call | solution.py:493
Async XLA Ops:
  0.6 0.8 %copy-start.1 = (bf16[16,8]{0,1:T(8,128)(2,1)S(1)}, bf16[16,8]{0,1:T(8,128)(2,1)}, u32[]{:S(2)}) copy-start(bf16[16,8]{0,1:T(8,128)(2,1)} %param.4) | copy-start | bytes 772
  1.4 1.2 %copy-start = (f32[64,32,128]{2,1,0:T(8,128)S(1)}, f32[64,32,128]{2,1,0:T(8,128)}, u32[]{:S(2)}) copy-start(f32[64,32,128]{2,1,0:T(8,128)} %param.3) | copy-start | bytes 3145732

commit v6 on v5

--- a/solution.py
+++ b/solution.py
@@ -25,15 +25,13 @@
     return jnp.maximum(v, lax.log2(1.0 + jnp.exp2(jnp.minimum(v, 126.0))))
 
 
-def widen(big_ref, weights_ref, scale):
-    cols, rows = weights_ref.shape
+def widen(big_ref, weights, scale):
+    rows, cols = weights.shape
     up = lax.broadcasted_iota(jnp.int32, (8 * rows, rows), 0) >> 3
     up = (up == lax.broadcasted_iota(jnp.int32, (8 * rows, rows), 1)).astype(jnp.float32)
     out = lax.broadcasted_iota(jnp.int32, (cols, 8 * cols), 1) >> 3
     out = (out == lax.broadcasted_iota(jnp.int32, (cols, 8 * cols), 0)).astype(jnp.float32)
-    tall = lax.dot_general(
-        up.astype(jnp.bfloat16), weights_ref[...], (((1,), (1,)), ((), ())), preferred_element_type=jnp.float32
-    )
+    tall = jnp.dot(up.astype(jnp.bfloat16), weights, preferred_element_type=jnp.float32)
     wide = jnp.dot(tall.astype(jnp.bfloat16), out.astype(jnp.bfloat16), preferred_element_type=jnp.float32)
     at_row = lax.broadcasted_iota(jnp.int32, wide.shape, 0) & 7
     at_col = lax.broadcasted_iota(jnp.int32, wide.shape, 1) & 7
@@ -73,14 +71,16 @@
     for x in xs:
         for y in ys:
             pl.semaphore_signal(barrier, inc=1, device_id=(x, y), device_id_type=MESH)
-    lax.fori_loop(1, count_x, greet_x, 0)
-    lax.fori_loop(1, count_y, greet_y, 0)
+    for hop in range(1, count_x):
+        greet_x(hop, 0)
+    for hop in range(1, count_y):
+        greet_y(hop, 0)
 
     def plane(x):
         return f_ref[pl.ds(x, 64, stride=32), :]
 
-    widen(w1_ref, win_ref, 0.5)
-    widen(w2_ref, wout_ref, 1.0)
+    widen(w1_ref, jnp.transpose(win_ref[...].astype(jnp.float32)).astype(jnp.bfloat16), 0.5)
+    widen(w2_ref, wout_ref[...], 1.0)
     fetch.wait()
     for i in range(3):
         xs_ref[0, i] = plane(i)
@@ -136,6 +136,78 @@
             )
         )
         copies[-1].start()
+
+    lane = lanes_of()
+    seg = lax.broadcasted_iota(jnp.int32, (8, 128), 0)
+    z = lane & 63
+    half = lane >> 6
+    top = z == 0
+    bottom = z == 63
+    full_x = 32 * count_x
+    full_y = 128 * count_y
+    at_x = me_x * 32 + half * 16
+    at_y = me_y * 128 + seg * 16
+
+    def above(v):
+        return jnp.where(top, 0.0, pltpu.roll(v, 1, 1))
+
+    def below(v):
+        return jnp.where(bottom, 0.0, pltpu.roll(v, 127, 1))
+
+    def inside(xp, yp):
+        gy = at_y + yp
+        ok = (gy >= 0) & (gy < full_y)
+        if xp < 0:
+            ok = ok & (at_x + xp >= 0)
+        if xp > 15:
+            ok = ok & (at_x + xp < full_x)
+        return ok
+
+    def field(xp, yp):
+        return tb_ref[xp + 3, pl.ds(yp + 8, 8, stride=16), :]
+
+    def first(yp, cells, masked=True):
+        mid = {xp: field(xp, yp) for xp in sorted({c + o for c in cells for o in (-1, 0, 1)})}
+        for xp in cells:
+            c = mid[xp]
+            near = field(xp, yp - 1) + field(xp, yp + 1)
+            near = near + (mid[xp - 1] + mid[xp + 1]) + (above(c) + below(c))
+            s = 0.4 * c + 0.1 * near
+            s1_ref[xp + 2, yp + 2] = jnp.where(inside(xp, yp), s, 0.0) if masked else s
+
+    def second(yp, cells, masked=True):
+        mid = {xp: s1_ref[xp + 2, yp + 2] for xp in sorted({c + o for c in cells for o in (-1, 0, 1)})}
+        around = [above(mid[xp]) + below(mid[xp]) for xp in cells]
+        rows = []
+        for xp, ends in zip(cells, around):
+            c = mid[xp]
+            near = s1_ref[xp + 2, yp + 1] + s1_ref[xp + 2, yp + 3]
+            near = near + (mid[xp - 1] + mid[xp + 1]) + ends
+            s = 0.4 * c + 0.1 * near
+            rows.append(jnp.where(inside(xp, yp), s, 0.0) if masked else s)
+        ups = [above(s) for s in rows]
+        downs = [below(s) for s in rows]
+        for xp, s, up, down in zip(cells, rows, ups, downs):
+            p_ref[xp + 1, yp + 1] = s
+            b_ref[xp + 1, yp + 1] = 2.0 * s + (up + down)
+            d_ref[xp + 1, yp + 1] = down - up
+
+    inner_first, outer_first = range(1, 15), (-2, -1, 0, 15, 16, 17)
+    inner_second, outer_second = range(2, 14), (-1, 0, 1, 14, 15, 16)
+    all_first, all_second = range(-2, 18), range(-1, 17)
+
+    def early_first(i, carry):
+        for n in range(7):
+            first(1 + 7 * i + n, inner_first, False)
+        return carry
+
+    def early_second(i, carry):
+        for n in range(2):
+            second(2 + 2 * i + n, inner_second, False)
+        return carry
+
+    lax.fori_loop(0, 2, early_first, 0)
+    lax.fori_loop(0, 6, early_second, 0)
 
     inner_x = (me_x > 0, me_x < count_x - 1)
     inner_y = (me_y > 0, me_y < count_y - 1)
@@ -161,55 +233,6 @@
     for copy in copies:
         copy.wait_send()
 
-    lane = lanes_of()
-    seg = lax.broadcasted_iota(jnp.int32, (8, 128), 0)
-    z = lane & 63
-    half = lane >> 6
-    top = z == 0
-    bottom = z == 63
-    full_x = 32 * count_x
-    full_y = 128 * count_y
-    at_x = me_x * 32 + half * 16
-    at_y = me_y * 128 + seg * 16
-
-    def above(v):
-        return jnp.where(top, 0.0, pltpu.roll(v, 1, 1))
-
-    def below(v):
-        return jnp.where(bottom, 0.0, pltpu.roll(v, 127, 1))
-
-    def inside(xp, yp):
-        gy = at_y + yp
-        ok = (gy >= 0) & (gy < full_y)
-        if xp < 0:
-            ok = ok & (at_x + xp >= 0)
-        if xp > 15:
-            ok = ok & (at_x + xp < full_x)
-        return ok
-
-    def field(xp, yp):
-        return tb_ref[xp + 3, pl.ds(yp + 8, 8, stride=16), :]
-
-    def first(yp):
-        mid = [field(xp, yp) for xp in range(-3, 19)]
-        for k in range(20):
-            c = mid[k + 1]
-            near = field(k - 2, yp - 1) + field(k - 2, yp + 1)
-            near = near + (mid[k] + mid[k + 2]) + (above(c) + below(c))
-            s1_ref[k, yp + 2] = jnp.where(inside(k - 2, yp), 0.4 * c + 0.1 * near, 0.0)
-
-    def second(yp):
-        mid = [s1_ref[k, yp + 2] for k in range(20)]
-        for k in range(18):
-            c = mid[k + 1]
-            near = s1_ref[k + 1, yp + 1] + s1_ref[k + 1, yp + 3]
-            near = near + (mid[k] + mid[k + 2]) + (above(c) + below(c))
-            s = jnp.where(inside(k - 1, yp), 0.4 * c + 0.1 * near, 0.0)
-            up, down = above(s), below(s)
-            p_ref[k, yp + 1] = s
-            b_ref[k, yp + 1] = 2.0 * s + (up + down)
-            d_ref[k, yp + 1] = down - up
-
     one = jnp.ones((8, 128), jnp.float32)
     zero = jnp.zeros((8, 128), jnp.float32)
 
@@ -266,7 +289,7 @@
         image = jnp.transpose(jnp.concatenate(colour + clear, axis=0))
         j_ref[pl.ds(row, 64, stride=4), :] = image[0:64]
 
-    def column(k):
+    def column(k, cells):
         past = (k + 15) // 16
         deliver(past * (((k + 3) // 4 - 1) * 256 + (k + 3) % 4) + (1 - past) * 1024)
         state = [zero] * BANDS + [one] * BANDS
@@ -274,8 +297,9 @@
             views(g, state)
             second_layer((g + 2) % chunks)
             first_layer((g + 4) % chunks, k + (g + 4) // chunks)
-        second(k + 3)
-        first(k + 5)
+        if cells:
+            second(k + 3, cells[1])
+            first(k + 5, cells[0])
         for b in range(2 * BANDS):
             st_ref[b] = state[b]
 
@@ -322,9 +346,9 @@
         )
 
     for yp in range(-2, 5):
-        first(yp)
+        first(yp, all_first if yp < 1 else outer_first)
     for yp in range(-1, 3):
-        second(yp)
+        second(yp, all_second if yp < 2 else outer_second)
     for b in range(BANDS):
         yc_ref[b] = jnp.zeros((128, 128), jnp.float32)
         yt_ref[b] = jnp.ones((128, 128), jnp.float32)
@@ -333,18 +357,22 @@
     for g in range(2):
         second_layer(g)
 
-    def one_column(k, carry):
-        column(k)
-
-        @pl.when((k > 0) & (k % 4 == 0))
-        def _():
-            send_slabs(k // 4 - 1)
-
-        return carry
-
-    lax.fori_loop(0, 16, one_column, 0)
+    def run(begin, end, cells):
+        def one_column(k, carry):
+            column(k, cells)
+
+            @pl.when((k > 0) & (k % 4 == 0))
+            def _():
+                send_slabs(k // 4 - 1)
+
+            return carry
+
+        lax.fori_loop(begin, end, one_column, 0)
+
+    run(0, 10, (outer_first, outer_second))
+    run(10, 14, (all_first, all_second))
+    run(14, 16, None)
     deliver(3 * 256 + 3)
-    send_slabs(3)
 
     for b in range(BANDS):
         for h in range(2):
@@ -374,7 +402,9 @@
         ).start()
         return carry
 
-    lax.fori_loop(1, count_y, send_rows, 0)
+    for hop in range(1, count_y):
+        send_rows(hop, 0)
+    send_slabs(3)
     rr_ref[me_y] = r_ref[me_y]
 
     at_ref[...] = jnp.zeros_like(at_ref)
@@ -505,7 +535,7 @@
     count_x = lax.axis_size("bx")
     count_y = lax.axis_size("by")
     ax, ay = march_call(
-        scalar_field.reshape(2048, 128), transfer_in.T, transfer_out.T, count_x, count_y
+        pltpu.with_memory_space_constraint(scalar_field.reshape(2048, 128), pltpu.HBM), transfer_in.T, transfer_out, count_x, count_y
     )
     vx, vy = emit_call(ax, ay)
     return (vx.reshape(2, 8, 2, 128), vy.reshape(2, 8, 8, 32))

time: 43.4 us -> 42 us (0.968)
  Pallas kernels: 40.6 us -> 39.7 us
  local copies, waits for them, and re-layouts: 2 us -> 1.36 us
    pallas_call x1, Pallas kernels: 39.9 us -> 39.1 us  [march_call(): pl.pallas_call(functools.partial(march, count_x, count_y), out_shape=(jax...]
    unnamed x5 -> x4, local copies, waits for them, and re-layouts: 2 us -> 1.36 us
where the time goes in v6:
time: 42 us; the launch traced here: 41.8 us
  Pallas kernels  39.7 us (95%)
  local copies, waits for them, and re-layouts  1.36 us (3%)
  between operations  0.65 us (2%)
    pallas_call x1, Pallas kernels, march_call(): pl.pallas_call(functools.partial(march, count_x, count_y), out_shape=(jax...  39.1 us
    unnamed x4, local copies, waits for them, and re-layouts  1.36 us

profile of v6, /device:TPU:1, one launch (start us, length us, event | category | flops | bytes accessed | tf_op | source)
XLA Modules:
  0.0 41.8 jit_solution(17925974090897806912)
XLA Ops:
  0.6 0.0 copy-start.1
  0.6 0.7 %copy-done.1 = bf16[16,8]{0,1:T(8,128)(2,1)S(1)} copy-done((bf16[16,8]{0,1:T(8,128)(2,1)S(1)}, bf16[16,8]{0,1:T(8,128)(2,1)}, u32[]{:S(2)}) %copy-start.1) | copy-done | bytes 280
  1.3 0.0 copy-start
  1.3 0.7 %copy-done = bf16[16,16]{1,0:T(8,128)(2,1)S(1)} copy-done((bf16[16,16]{1,0:T(8,128)(2,1)S(1)}, bf16[16,16]{1,0:T(8,128)(2,1)}, u32[]{:S(2)}) %copy-start) | copy-done | bytes 536
  2.0 39.1 %march.1 = (f32[16,2,128]{2,1,0:T(2,128)S(1)}, f32[16,8,32]{2,1,0:T(8,128)S(1)}) custom-call(f32[2048,128]{1,0:T(8,128)} %bitcast.5, bf16[8,16]{1,0:T(8,128)(2,1)S(1)} %bitcast.4, bf16[16,16]{1,0:T(8,128)(2,1)S(1)} %copy-done), custom_call_target="tpu_custom_call" | custom-call | tf_op jit(solution)/shard_map/march/pallas_call | solution.py:463
  41.1 0.7 %emit.1 = (f32[16,2,128]{2,1,0:T(2,128)}, f32[16,8,32]{2,1,0:T(8,128)}) custom-call(f32[16,2,128]{2,1,0:T(2,128)S(1)} %get-tuple-element.6.ax_ref, f32[16,8,32]{2,1,0:T(8,128)S(1)} %get-tuple-element.7.ay_ref), custom_call_target="tpu_custom_call" | custom-call | tf_op jit(solution)/shard_map/emit/pallas_call | solution.py:523
Async XLA Ops:
  0.6 0.7 %copy-start.1 = (bf16[16,8]{0,1:T(8,128)(2,1)S(1)}, bf16[16,8]{0,1:T(8,128)(2,1)}, u32[]{:S(2)}) copy-start(bf16[16,8]{0,1:T(8,128)(2,1)} %param.4) | copy-start | bytes 772
  1.3 0.7 %copy-start = (bf16[16,16]{1,0:T(8,128)(2,1)S(1)}, bf16[16,16]{1,0:T(8,128)(2,1)}, u32[]{:S(2)}) copy-start(bf16[16,16]{1,0:T(8,128)(2,1)} %wout_ref.1) | copy-start | bytes 1540

commit v7 on v6

--- a/solution.py
+++ b/solution.py
@@ -21,7 +21,6 @@
 
 
 def softplus(v):
-    v = v * LOG2E
     return jnp.maximum(v, lax.log2(1.0 + jnp.exp2(jnp.minimum(v, 126.0))))
 
 
@@ -35,14 +34,18 @@
     wide = jnp.dot(tall.astype(jnp.bfloat16), out.astype(jnp.bfloat16), preferred_element_type=jnp.float32)
     at_row = lax.broadcasted_iota(jnp.int32, wide.shape, 0) & 7
     at_col = lax.broadcasted_iota(jnp.int32, wide.shape, 1) & 7
-    big_ref[...] = jnp.where(at_row == at_col, wide * scale, 0.0).astype(jnp.bfloat16)
+    wide = jnp.where(at_row == at_col, wide * scale, 0.0)
+    big_ref[:, 0 : wide.shape[1]] = wide.astype(jnp.bfloat16)
+    if big_ref.shape[1] > wide.shape[1]:
+        wide = wide - wide.astype(jnp.bfloat16).astype(jnp.float32)
+        big_ref[:, wide.shape[1] :] = wide.astype(jnp.bfloat16)
 
 
 def march(
-    count_x, count_y, field_ref, win_ref, wout_ref, vx_ref, vy_ref,
+    count_x, count_y, field_ref, win_hbm, wout_hbm, vx_ref, vy_ref,
     tb_ref, xs_ref, xr_ref, yr_ref, cr_ref,
     w1_ref, w2_ref, s1_ref, p_ref, b_ref, d_ref, x_ref, u_ref, ch_ref, yc_ref, yt_ref, rs_ref,
-    j_ref, jr_ref, r_ref, rr_ref, at_ref, st_ref, f_ref, load,
+    j_ref, jr_ref, r_ref, rr_ref, at_ref, st_ref, f_ref, win_ref, wout_ref, load,
     sx, rx, sy, ry, sc, rc, send_x, recv_x, send_y, recv_y,
 ):
     me_x = lax.axis_index("bx")
@@ -56,8 +59,13 @@
     def peer_y(hop):
         return lax.rem(me_y + hop, count_y)
 
-    fetch = pltpu.make_async_copy(field_ref, f_ref, load)
-    fetch.start()
+    fetches = (
+        pltpu.make_async_copy(win_hbm, win_ref, load.at[0]),
+        pltpu.make_async_copy(wout_hbm, wout_ref, load.at[1]),
+        pltpu.make_async_copy(field_ref, f_ref, load.at[2]),
+    )
+    for fetch in fetches:
+        fetch.start()
     barrier = pltpu.get_barrier_semaphore()
 
     def greet_x(hop, carry):
@@ -79,9 +87,11 @@
     def plane(x):
         return f_ref[pl.ds(x, 64, stride=32), :]
 
+    fetches[0].wait()
+    fetches[1].wait()
     widen(w1_ref, jnp.transpose(win_ref[...].astype(jnp.float32)).astype(jnp.bfloat16), 0.5)
-    widen(w2_ref, wout_ref[...], 1.0)
-    fetch.wait()
+    widen(w2_ref, wout_ref[...], LOG2E)
+    fetches[2].wait()
     for i in range(3):
         xs_ref[0, i] = plane(i)
         xs_ref[1, i] = plane(29 + i)
@@ -261,6 +271,7 @@
         slot = g
         u = u_ref[slot]
         hidden = (u + u * jnp.tanh(u)).astype(jnp.bfloat16)
+        hidden = jnp.concatenate([hidden, hidden], axis=0)
         ch_ref[slot] = jnp.dot(w2_ref[...], hidden, preferred_element_type=jnp.float32)
 
     def views(g, state):
@@ -466,7 +477,7 @@
             jax.ShapeDtypeStruct((16, 2, 128), jnp.float32),
             jax.ShapeDtypeStruct((16, 8, 32), jnp.float32),
         ),
-        in_specs=[pl.BlockSpec(memory_space=pltpu.HBM), vmem, vmem],
+        in_specs=[pl.BlockSpec(memory_space=pltpu.HBM)] * 3,
         out_specs=(vmem, vmem),
         scratch_shapes=[
             held(22, 144, 128),
@@ -475,7 +486,7 @@
             held(2, 16, 8, 128),
             held(4, 3, 8, 128),
             held(128, 64, dtype=jnp.bfloat16),
-            held(128, 128, dtype=jnp.bfloat16),
+            held(128, 256, dtype=jnp.bfloat16),
             held(20, 23, 8, 128),
             held(18, 20, 8, 128),
             held(18, 20, 8, 128),
@@ -493,7 +504,9 @@
             held(128, 128),
             held(16, 8, 128),
             held(2048, 128),
-            pltpu.SemaphoreType.DMA,
+            held(8, 16, dtype=jnp.bfloat16),
+            held(16, 16, dtype=jnp.bfloat16),
+            pltpu.SemaphoreType.DMA((3,)),
             pltpu.SemaphoreType.DMA((2,)),
             pltpu.SemaphoreType.DMA((2,)),
             pltpu.SemaphoreType.DMA((2,)),
@@ -535,7 +548,11 @@
     count_x = lax.axis_size("bx")
     count_y = lax.axis_size("by")
     ax, ay = march_call(
-        pltpu.with_memory_space_constraint(scalar_field.reshape(2048, 128), pltpu.HBM), transfer_in.T, transfer_out, count_x, count_y
+        pltpu.with_memory_space_constraint(scalar_field.reshape(2048, 128), pltpu.HBM),
+        pltpu.with_memory_space_constraint(transfer_in.T, pltpu.HBM),
+        pltpu.with_memory_space_constraint(transfer_out, pltpu.HBM),
+        count_x,
+        count_y,
     )
     vx, vy = emit_call(ax, ay)
     return (vx.reshape(2, 8, 2, 128), vy.reshape(2, 8, 8, 32))

time: 42 us -> 41.1 us (0.979)
  local copies, waits for them, and re-layouts: 1.36 us -> 0 us
    unnamed x4 -> x0, local copies, waits for them, and re-layouts: 1.36 us -> none
where the time goes in v7:
time: 41.1 us; the launch traced here: 40.5 us
  Pallas kernels  39.8 us (97%)
  between operations  0.64 us (2%)
    pallas_call x1, Pallas kernels, march_call(): pl.pallas_call(functools.partial(march, count_x, count_y), out_shape=(jax...  39.2 us

profile of v7, /device:TPU:1, one launch (start us, length us, event | category | flops | bytes accessed | tf_op | source)
XLA Modules:
  0.0 40.5 jit_solution(7732673899781833788)
XLA Ops:
  0.6 39.2 %march.1 = (f32[16,2,128]{2,1,0:T(2,128)S(1)}, f32[16,8,32]{2,1,0:T(8,128)S(1)}) custom-call(f32[2048,128]{1,0:T(8,128)} %bitcast.4, bf16[8,16]{1,0:T(8,128)(2,1)} %bitcast.5, bf16[16,16]{1,0:T(8,128)(2,1)} %wout_hbm.1), custom_call_target="tpu_custom_call" | custom-call | tf_op jit(solution)/shard_map/march/pallas_call | solution.py:474
  39.8 0.7 %emit.1 = (f32[16,2,128]{2,1,0:T(2,128)}, f32[16,8,32]{2,1,0:T(8,128)}) custom-call(f32[16,2,128]{2,1,0:T(2,128)S(1)} %get-tuple-element.6.ax_ref, f32[16,8,32]{2,1,0:T(8,128)S(1)} %get-tuple-element.7.ay_ref), custom_call_target="tpu_custom_call" | custom-call | tf_op jit(solution)/shard_map/emit/pallas_call | solution.py:536

commit v8 on v7

--- a/solution.py
+++ b/solution.py
@@ -13,7 +13,7 @@
 LOG2E = 1.4426950408889634
 LN2 = 0.6931471805599453
 MESH = pl.DeviceIdType.MESH
-GROUP = 4
+GROUP = 2
 
 
 def lanes_of():
@@ -305,9 +305,9 @@
         deliver(past * (((k + 3) // 4 - 1) * 256 + (k + 3) % 4) + (1 - past) * 1024)
         state = [zero] * BANDS + [one] * BANDS
         for g in range(chunks):
+            first_layer((g + 8) % chunks, k + (g + 8) // chunks)
             views(g, state)
-            second_layer((g + 2) % chunks)
-            first_layer((g + 4) % chunks, k + (g + 4) // chunks)
+            second_layer((g + 4) % chunks)
         if cells:
             second(k + 3, cells[1])
             first(k + 5, cells[0])
@@ -330,7 +330,7 @@
             ).start()
             return carry
 
-        for hop in range(1, count_x):
+        for hop in sorted(range(1, count_x), key=lambda h: abs(h - count_x // 2)):
             one_peer(hop, 0)
         jr_ref[slab(c * 256 + me_x * 8), :] = j_ref[slab(c * 256 + me_x * 8), :]
 
@@ -363,9 +363,9 @@
     for b in range(BANDS):
         yc_ref[b] = jnp.zeros((128, 128), jnp.float32)
         yt_ref[b] = jnp.ones((128, 128), jnp.float32)
+    for g in range(8):
+        first_layer(g, 0)
     for g in range(4):
-        first_layer(g, 0)
-    for g in range(2):
         second_layer(g)
 
     def run(begin, end, cells):
@@ -413,7 +413,7 @@
         ).start()
         return carry
 
-    for hop in range(1, count_y):
+    for hop in sorted(range(1, count_y), key=lambda h: abs(h - count_y // 2)):
         send_rows(hop, 0)
     send_slabs(3)
     rr_ref[me_y] = r_ref[me_y]

time: 41.1 us -> 39.6 us (0.964); the launches traced: 40.5 us -> 39.5 us
  Pallas kernels: 39.8 us -> 38.8 us
    pallas_call x1, Pallas kernels: 39.2 us -> 38.2 us  [march_call(): pl.pallas_call(functools.partial(march, count_x, count_y), out_shape=(jax...]
where the time goes in v8:
time: 39.6 us; the launch traced here: 39.5 us
  Pallas kernels  38.8 us (98%)
  between operations  0.64 us (2%)
    pallas_call x1, Pallas kernels, march_call(): pl.pallas_call(functools.partial(march, count_x, count_y), out_shape=(jax...  38.2 us

profile of v8, /device:TPU:1, one launch (start us, length us, event | category | flops | bytes accessed | tf_op | source)
XLA Modules:
  0.0 39.5 jit_solution(15944497930929529135)
XLA Ops:
  0.6 38.2 %march.1 = (f32[16,2,128]{2,1,0:T(2,128)S(1)}, f32[16,8,32]{2,1,0:T(8,128)S(1)}) custom-call(f32[2048,128]{1,0:T(8,128)} %bitcast.4, bf16[8,16]{1,0:T(8,128)(2,1)} %bitcast.5, bf16[16,16]{1,0:T(8,128)(2,1)} %wout_hbm.1), custom_call_target="tpu_custom_call" | custom-call | tf_op jit(solution)/shard_map/march/pallas_call | solution.py:474
  38.8 0.7 %emit.1 = (f32[16,2,128]{2,1,0:T(2,128)}, f32[16,8,32]{2,1,0:T(8,128)}) custom-call(f32[16,2,128]{2,1,0:T(2,128)S(1)} %get-tuple-element.6.ax_ref, f32[16,8,32]{2,1,0:T(8,128)S(1)} %get-tuple-element.7.ay_ref), custom_call_target="tpu_custom_call" | custom-call | tf_op jit(solution)/shard_map/emit/pallas_call | solution.py:536

commit v9 on v8

--- a/solution.py
+++ b/solution.py
@@ -62,7 +62,9 @@
     fetches = (
         pltpu.make_async_copy(win_hbm, win_ref, load.at[0]),
         pltpu.make_async_copy(wout_hbm, wout_ref, load.at[1]),
-        pltpu.make_async_copy(field_ref, f_ref, load.at[2]),
+    ) + tuple(
+        pltpu.make_async_copy(field_ref.at[pl.ds(256 * n, 256)], f_ref.at[pl.ds(256 * n, 256)], load.at[2 + n])
+        for n in range(8)
     )
     for fetch in fetches:
         fetch.start()
@@ -91,7 +93,8 @@
     fetches[1].wait()
     widen(w1_ref, jnp.transpose(win_ref[...].astype(jnp.float32)).astype(jnp.bfloat16), 0.5)
     widen(w2_ref, wout_ref[...], LOG2E)
-    fetches[2].wait()
+    for fetch in fetches[2:]:
+        fetch.wait()
     for i in range(3):
         xs_ref[0, i] = plane(i)
         xs_ref[1, i] = plane(29 + i)
@@ -506,7 +509,7 @@
             held(2048, 128),
             held(8, 16, dtype=jnp.bfloat16),
             held(16, 16, dtype=jnp.bfloat16),
-            pltpu.SemaphoreType.DMA((3,)),
+            pltpu.SemaphoreType.DMA((10,)),
             pltpu.SemaphoreType.DMA((2,)),
             pltpu.SemaphoreType.DMA((2,)),
             pltpu.SemaphoreType.DMA((2,)),

time: 39.6 us -> 39.6 us (level)
  no operation moved by 1% of the time
where the time goes in v9:
time: 39.6 us; the launch traced here: 39.5 us
  Pallas kernels  38.9 us (98%)
  between operations  0.64 us (2%)
    pallas_call x1, Pallas kernels, march_call(): pl.pallas_call(functools.partial(march, count_x, count_y), out_shape=(jax...  38.2 us

profile of v9, /device:TPU:1, one launch (start us, length us, event | category | flops | bytes accessed | tf_op | source)
XLA Modules:
  0.0 39.5 jit_solution(10492423895097636424)
XLA Ops:
  0.6 38.2 %march.1 = (f32[16,2,128]{2,1,0:T(2,128)S(1)}, f32[16,8,32]{2,1,0:T(8,128)S(1)}) custom-call(f32[2048,128]{1,0:T(8,128)} %bitcast.4, bf16[8,16]{1,0:T(8,128)(2,1)} %bitcast.5, bf16[16,16]{1,0:T(8,128)(2,1)} %wout_hbm.1), custom_call_target="tpu_custom_call" | custom-call | tf_op jit(solution)/shard_map/march/pallas_call | solution.py:477
  38.8 0.7 %emit.1 = (f32[16,2,128]{2,1,0:T(2,128)}, f32[16,8,32]{2,1,0:T(8,128)}) custom-call(f32[16,2,128]{2,1,0:T(2,128)S(1)} %get-tuple-element.6.ax_ref, f32[16,8,32]{2,1,0:T(8,128)S(1)} %get-tuple-element.7.ay_ref), custom_call_target="tpu_custom_call" | custom-call | tf_op jit(solution)/shard_map/emit/pallas_call | solution.py:539

commit v10 on v8

--- a/solution.py
+++ b/solution.py
@@ -87,10 +87,6 @@
     def plane(x):
         return f_ref[pl.ds(x, 64, stride=32), :]
 
-    fetches[0].wait()
-    fetches[1].wait()
-    widen(w1_ref, jnp.transpose(win_ref[...].astype(jnp.float32)).astype(jnp.bfloat16), 0.5)
-    widen(w2_ref, wout_ref[...], LOG2E)
     fetches[2].wait()
     for i in range(3):
         xs_ref[0, i] = plane(i)
@@ -221,13 +217,20 @@
 
     inner_x = (me_x > 0, me_x < count_x - 1)
     inner_y = (me_y > 0, me_y < count_y - 1)
-    copies[0].wait_recv()
-    copies[1].wait_recv()
+    fetches[0].wait()
+    fetches[1].wait()
+    widen(w1_ref, jnp.transpose(win_ref[...].astype(jnp.float32)).astype(jnp.bfloat16), 0.5)
+    widen(w2_ref, wout_ref[...], LOG2E)
+    for b in range(BANDS):
+        yc_ref[b] = jnp.zeros((128, 128), jnp.float32)
+        yt_ref[b] = jnp.ones((128, 128), jnp.float32)
+    at_ref[...] = jnp.zeros_like(at_ref)
+
+    for copy in copies:
+        copy.wait_recv()
     for i in range(3):
         turn(i - 3, jnp.where(inner_x[0], xr_ref[0, i], 0.0), plane(13 + i))
         turn(16 + i, plane(16 + i), jnp.where(inner_x[1], xr_ref[1, i], 0.0))
-    for copy in copies[2:]:
-        copy.wait_recv()
     low = lanes_of() < 64
     rims = (pl.ds(0, 8), pl.ds(136, 8))
     for part in range(2):
@@ -360,9 +363,6 @@
         first(yp, all_first if yp < 1 else outer_first)
     for yp in range(-1, 3):
         second(yp, all_second if yp < 2 else outer_second)
-    for b in range(BANDS):
-        yc_ref[b] = jnp.zeros((128, 128), jnp.float32)
-        yt_ref[b] = jnp.ones((128, 128), jnp.float32)
     for g in range(8):
         first_layer(g, 0)
     for g in range(4):
@@ -418,7 +418,6 @@
     send_slabs(3)
     rr_ref[me_y] = r_ref[me_y]
 
-    at_ref[...] = jnp.zeros_like(at_ref)
 
     def fold_x(c):
         slabs_moved(c).wait_recv()

time: 39.6 us -> 39.7 us (level)
  no operation moved by 1% of the time
where the time goes in v10:
time: 39.7 us; the launch traced here: 39.5 us
  Pallas kernels  38.9 us (98%)
  between operations  0.64 us (2%)
    pallas_call x1, Pallas kernels, march_call(): pl.pallas_call(functools.partial(march, count_x, count_y), out_shape=(jax...  38.3 us

profile of v10, /device:TPU:1, one launch (start us, length us, event | category | flops | bytes accessed | tf_op | source)
XLA Modules:
  0.0 39.5 jit_solution(11557539750803904568)
XLA Ops:
  0.6 38.3 %march.1 = (f32[16,2,128]{2,1,0:T(2,128)S(1)}, f32[16,8,32]{2,1,0:T(8,128)S(1)}) custom-call(f32[2048,128]{1,0:T(8,128)} %bitcast.4, bf16[8,16]{1,0:T(8,128)(2,1)} %bitcast.5, bf16[16,16]{1,0:T(8,128)(2,1)} %wout_hbm.1), custom_call_target="tpu_custom_call" | custom-call | tf_op jit(solution)/shard_map/march/pallas_call | solution.py:473
  38.9 0.7 %emit.1 = (f32[16,2,128]{2,1,0:T(2,128)}, f32[16,8,32]{2,1,0:T(8,128)}) custom-call(f32[16,2,128]{2,1,0:T(2,128)S(1)} %get-tuple-element.6.ax_ref, f32[16,8,32]{2,1,0:T(8,128)S(1)} %get-tuple-element.7.ay_ref), custom_call_target="tpu_custom_call" | custom-call | tf_op jit(solution)/shard_map/emit/pallas_call | solution.py:535

commit v11 on v10

--- a/solution.py
+++ b/solution.py
@@ -384,6 +384,7 @@
     run(10, 14, (all_first, all_second))
     run(14, 16, None)
     deliver(3 * 256 + 3)
+    send_slabs(3)
 
     for b in range(BANDS):
         for h in range(2):
@@ -415,7 +416,6 @@
 
     for hop in sorted(range(1, count_y), key=lambda h: abs(h - count_y // 2)):
         send_rows(hop, 0)
-    send_slabs(3)
     rr_ref[me_y] = r_ref[me_y]
 
 

time: 39.7 us -> 39.7 us (level)
  no operation moved by 1% of the time
where the time goes in v11:
time: 39.7 us; the launch traced here: 39.6 us
  Pallas kernels  38.9 us (98%)
  between operations  0.64 us (2%)
    pallas_call x1, Pallas kernels, march_call(): pl.pallas_call(functools.partial(march, count_x, count_y), out_shape=(jax...  38.3 us

profile of v11, /device:TPU:1, one launch (start us, length us, event | category | flops | bytes accessed | tf_op | source)
XLA Modules:
  0.0 39.6 jit_solution(4196411354762352278)
XLA Ops:
  0.6 38.3 %march.1 = (f32[16,2,128]{2,1,0:T(2,128)S(1)}, f32[16,8,32]{2,1,0:T(8,128)S(1)}) custom-call(f32[2048,128]{1,0:T(8,128)} %bitcast.4, bf16[8,16]{1,0:T(8,128)(2,1)} %bitcast.5, bf16[16,16]{1,0:T(8,128)(2,1)} %wout_hbm.1), custom_call_target="tpu_custom_call" | custom-call | tf_op jit(solution)/shard_map/march/pallas_call | solution.py:473
  38.9 0.7 %emit.1 = (f32[16,2,128]{2,1,0:T(2,128)}, f32[16,8,32]{2,1,0:T(8,128)}) custom-call(f32[16,2,128]{2,1,0:T(2,128)S(1)} %get-tuple-element.6.ax_ref, f32[16,8,32]{2,1,0:T(8,128)S(1)} %get-tuple-element.7.ay_ref), custom_call_target="tpu_custom_call" | custom-call | tf_op jit(solution)/shard_map/emit/pallas_call | solution.py:535
